TPU v7x, 32 devices: a whole 2x2x4 slice. The times are simulated.
32 devices in a mesh: dp: 8 (over y, x, core), group: 4 (over z).
Axes of the slice: x: 2, y: 2, z: 4, core: 2. Of those that a mesh axis runs over, the one named last changes fastest.
Arguments:
- images: bfloat16 [64, 196, 512], P(('dp', 'group')), may hold values from -6 to 6
- grad_output: bfloat16 [64, 196, 512], P(('dp', 'group')), may hold values from -6 to 6
- live_count: int32 [8, 4], P('dp', 'group'), may hold values from 1 to 2, as said below
- qkv_weight: float32 [512, 1536], P(None, 'group'), may hold values from -0.25 to 0.25
- proj_weight: float32 [512, 512], P(None, 'group'), may hold values from -0.75 to 0.75
- up_weight: float32 [512, 2048], P(None, 'group'), may hold values from -0.25 to 0.25
- down_weight: float32 [2048, 512], P('group'), may hold values from -0.125 to 0.125
- qkv_moment: float32 [512, 1536], P(None, 'group'), may hold values from -360 to 360
- proj_moment: float32 [512, 512], P(None, 'group'), may hold values from -360 to 360
- up_moment: float32 [512, 2048], P(None, 'group'), may hold values from -360 to 360
- down_moment: float32 [2048, 512], P('group'), may hold values from -360 to 360
- vectors: float32 [8, 512], replicated
- hidden_bias: float32 [2048], replicated, may hold values from -2 to 2
- rel_table: float32 [169, 16], replicated, may hold values from -4 to 4
- vector_first: float32 [8, 512], replicated, may hold values from -30 to 30
- vector_second: float32 [8, 512], replicated, may hold values from 1 to 30
- bias_first: float32 [2048], replicated, may hold values from -30 to 30
- bias_second: float32 [2048], replicated, may hold values from 1 to 30
- table_first: float32 [169, 16], replicated, may hold values from -30 to 30
- table_second: float32 [169, 16], replicated, may hold values from 1 to 30
Outputs:
- output: bfloat16 [64, 196, 512], P(('dp', 'group'))
- input_grad: float32 [64, 196, 512], P(('dp', 'group'))
- qkv_grad: float32 [512, 1536], P(None, 'group')
- proj_grad: float32 [512, 512], P(None, 'group')
- up_grad: float32 [512, 2048], P(None, 'group')
- down_grad: float32 [2048, 512], P('group')
- vector_grad: float32 [8, 512], replicated
- bias_grad: float32 [2048], replicated
- table_grad: float32 [169, 16], replicated
- new_qkv: float32 [512, 1536], P(None, 'group')
- new_proj: float32 [512, 512], P(None, 'group')
- new_up: float32 [512, 2048], P(None, 'group')
- new_down: float32 [2048, 512], P('group')
- qkv_momentum: float32 [512, 1536], P(None, 'group')
- proj_momentum: float32 [512, 512], P(None, 'group')
- up_momentum: float32 [512, 2048], P(None, 'group')
- down_momentum: float32 [2048, 512], P('group')
- new_vectors: float32 [8, 512], replicated
- new_bias: float32 [2048], replicated
- new_table: float32 [169, 16], replicated
- vector_mean: float32 [8, 512], replicated
- vector_square: float32 [8, 512], replicated
- bias_mean: float32 [2048], replicated
- bias_square: float32 [2048], replicated
- table_mean: float32 [169, 16], replicated
- table_square: float32 [169, 16], replicated
Inputs may be any that keep to these rules, and one draw needn't show every extreme that they name: Each device holds live images in its first live_count slots; every device has at least one, and some device is full in every draw.
All inputs are finite; a program needn't handle non-finite values.
Results may differ from a plain program's by a relative error of at most 0.017.
Values may be sent and summed in bfloat16 or wider, within the bound.
No kernel may reach another device: no remote copies, remote signals or barrier semaphores. Data moves between devices by JAX's collectives and lax.ppermute only.
A program may use at most 128 MiB of HBM per device.

v0:
```python
import functools
import math

import jax
import jax.numpy as jnp
import numpy as np
from jax import lax
from jax.experimental import pallas as pl
from jax.experimental.pallas import tpu as pltpu
from jax.sharding import PartitionSpec as P

D = 512
FF = 2048
SIDE = 14
WIN = 7
SHIFT = 3
NS_STEPS = 5


norm_eps = 1e-05
mask_fill = -100.0
muon_momentum = 0.95
muon_rate = 0.4
muon_decay = 0.1
adam_rate = 0.1
beta_first = 0.9
beta_second = 0.999
adam_eps = 1e-08
adam_count = 10.0
frob_eps = 1e-06
newton_first = 3.4445
newton_second = -4.775
newton_third = 2.0315


def window_tables(side, window, shift):
    steps = np.arange(window)
    row_pos = np.repeat(steps, window)
    col_pos = np.tile(steps, window)
    span = 2 * window - 1
    offset = (row_pos[:, None] - row_pos[None, :] + window - 1) * span + (
        col_pos[:, None] - col_pos[None, :] + window - 1
    )
    onehot = (offset.reshape(-1)[:, None] == np.arange(span * span)[None, :]).astype(np.float32)
    line = np.arange(side)
    label = (line >= side - window).astype(np.int64) + (line >= side - shift).astype(np.int64)
    region = 3 * label[:, None] + label[None, :]
    per_side = side // window
    region = (
        region.reshape(per_side, window, per_side, window)
        .transpose(0, 2, 1, 3)
        .reshape(per_side * per_side, window * window)
    )
    blocked = np.where(region[:, :, None] != region[:, None, :], mask_fill, 0.0).astype(np.float32)
    return (jnp.asarray(onehot), jnp.asarray(blocked))


def norm_back(grad_scaled, scaled, inverse):
    centre = jnp.mean(grad_scaled, -1, keepdims=True)
    along = jnp.mean(grad_scaled * scaled, -1, keepdims=True)
    return inverse * (grad_scaled - centre - scaled * along)


BF = jnp.bfloat16
F32 = jnp.float32
HALF = D // 2
PART = D // 8


def shape(dims, kind):
    return jax.ShapeDtypeStruct(tuple(dims), kind)


def run(kernel, name, places, args, outs, scratch=(), flops=0):
    vmem = pl.BlockSpec(memory_space=pltpu.VMEM)
    moved = sum((int(np.prod(item.shape)) * item.dtype.itemsize for item in [*args, *outs]))
    return pl.pallas_call(
        kernel,
        out_shape=list(outs),
        in_specs=[pl.BlockSpec(memory_space=pltpu.SMEM)] + [vmem] * len(args),
        out_specs=[vmem] * len(outs),
        scratch_shapes=list(scratch),
        name=name,
        cost_estimate=pl.CostEstimate(flops=flops, bytes_accessed=moved, transcendentals=0),
        compiler_params=pltpu.CompilerParams(vmem_limit_bytes=62 * 1024 * 1024),
    )(places, *args)


def rows_at(start, size):
    return pl.ds(pl.multiple_of(start, size), size)


def prep_kernel(place, wq, wp, wu, wd, mq, mp, mu, md, sa, sb, pa, pb, mom, flip):
    ug, qg = (wu.shape[1], wq.shape[1])
    core, chip = (place[0], place[1])
    sb[:, :qg] = wq[...].astype(BF)
    sb[:, qg:] = wp[...].astype(BF)
    sa[:, :ug] = wu[...].astype(BF)
    sa[:, ug:] = wd[...].T.astype(BF)
    for half in range(2):
        bit = (chip >> half) & 1
        source = rows_at(half * HALF + (bit * 2 + core) * PART, PART)
        pa[half * PART : (half + 1) * PART, :] = sa[source, :]
        pb[half * PART : (half + 1) * PART, :] = sb[source, :]
    flip[...] = md[...].T
    piece = mom.shape[0]
    source = rows_at(core * HALF + chip * piece, piece)
    mom[:, :ug] = mu[source, :]
    mom[:, ug : 2 * ug] = flip[source, :]
    mom[:, 2 * ug : 2 * ug + qg] = mq[source, :]
    mom[:, 2 * ug + qg :] = mp[source, :]


def join_kernel(group_count, widths, place, *refs):
    core, chip, zone = (place[0], place[1], place[2])
    far = group_count - 1
    own = refs[0]
    mine = refs[1 : 1 + far] + refs[1 + far : 3 + far]
    theirs = refs[3 + far : 3 + 2 * far] + refs[3 + 2 * far : 5 + 2 * far]
    outs = refs[5 + 2 * far :]
    offset = 0
    for out, width in zip(outs, widths):
        span = slice(offset, offset + width)
        out[:, rows_at(zone * width, width)] = own[:, span]
        for step in range(1, group_count):
            columns = rows_at((zone ^ step) * width, width)
            for parts, seat in ((mine, core), (theirs, 1 - core)):
                for half in range(2):
                    bit = (chip >> half) & 1
                    base = half * HALF
                    near = parts[step - 1][half * PART : (half + 1) * PART, span]
                    out[rows_at(base + (bit * 2 + seat) * PART, PART), columns] = near
                    swap = parts[far + half][(step - 1) * PART : step * PART, span]
                    out[rows_at(base + ((1 - bit) * 2 + seat) * PART, PART), columns] = swap
        offset += width


def halve_kernel(place, keep, came, own, *sends):
    chip = place[1]
    piece = own.shape[0]

    def total(step):
        source = rows_at((chip ^ step) * piece, piece)
        return keep[source, :].astype(F32) + came[source, :].astype(F32)

    own[...] = total(0)
    for step, send in enumerate(sends):
        send[...] = total(step + 1).astype(BF)


def plane_kernel(chips, place, *refs):
    zone = place[2]
    own, came, outs = (refs[0], refs[1:chips], refs[chips:])
    width = outs[0].shape[1]

    def total(step):
        columns = rows_at((zone ^ step) * width, width)
        value = own[:, columns]
        for item in came:
            value = value + item[:, columns].astype(F32)
        return value

    outs[0][...] = total(0)
    for step in range(1, len(outs)):
        outs[step][...] = total(step).astype(BF)


def momentum_kernel(group_count, qg, place, *refs):
    zone = place[2]
    first = refs[:group_count]
    second = refs[group_count : 2 * group_count]
    mom, piece = refs[2 * group_count : 2 * group_count + 2]
    outs, slots = (refs[2 * group_count + 2 : -1], refs[-1])
    ug = slots.shape[2]

    def total(parts):
        value = parts[0][...]
        for item in parts[1:]:
            value = value + item[...].astype(F32)
        return value

    one, two = (total(first), total(second))
    piece[:, : 2 * ug] = one.astype(BF)
    piece[:, 2 * ug :] = two.astype(BF)
    one = muon_momentum * mom[:, : 2 * ug] + one
    two = muon_momentum * mom[:, 2 * ug :] + two
    slots[...] = jnp.zeros_like(slots)
    slots[0] = one[:, :ug].astype(BF)
    slots[1] = one[:, ug:].astype(BF)
    slots[2, :, :qg] = two[:, :qg].astype(BF)
    slots[3, :, : two.shape[1] - qg] = two[:, qg:].astype(BF)
    for step in range(group_count):
        outs[step][...] = slots[zone ^ step]


def split(value):
    high = value.astype(BF)
    return (high, (value - high.astype(F32)).astype(BF))


def dot32(left, right):
    return jnp.dot(left, right, preferred_element_type=F32)


def triple(left, right):
    return dot32(left[0], right[0]) + (dot32(left[0], right[1]) + dot32(left[1], right[0]))


def newton_kernel(count, place, *refs):
    parts, outs = (refs[:count], refs[count:-3])
    whole, gram, lead = refs[-3:]
    piece = parts[0].shape[0]
    for step, item in enumerate(parts):
        whole[step * piece : (step + 1) * piece, :] = item[...]
    matrix = whole[...]
    raw = lax.dot_general(matrix, matrix, (((1,), (1,)), ((), ())), preferred_element_type=F32)
    row = lax.broadcasted_iota(jnp.int32, raw.shape, 0)
    column = lax.broadcasted_iota(jnp.int32, raw.shape, 1)
    norm = jnp.sqrt(jnp.sum(jnp.where(row == column, raw, 0.0), keepdims=True))
    scale = 1.0 / (norm + frob_eps)
    gram[...] = raw * (scale * scale)
    lead[...] = jnp.where(row[:piece] == column[:piece], scale, 0.0)

    def sweep(index, carry):
        now = gram[...]
        pair = split(now)
        square = triple(pair, pair)
        poly = newton_second * now + newton_third * square
        front = lead[...]
        turn = split(poly)
        lead[...] = newton_first * front + triple(split(front), turn)
        mixed = newton_first * now + triple(turn, pair)
        gram[...] = newton_first * mixed + triple(turn, split(mixed))
        return carry

    lax.fori_loop(0, NS_STEPS - 1, sweep, 0)
    pair = split(gram[...])
    front = lead[...]
    once = triple(split(front), pair)
    twice = newton_second * front + newton_third * once
    front = newton_first * front + triple(split(twice), pair)
    high, low = split(front)
    width = outs[0].shape[1]
    for step, out in enumerate(outs):
        block = whole[:, step * width : (step + 1) * width]
        out[...] = (dot32(high, block) + dot32(low, block)).astype(BF)


def pack_kernel(group_count, qg, place, *refs):
    zone = place[2]
    out, stack = refs[group_count:]
    ug = stack.shape[2]
    for step in range(group_count):
        stack[step] = refs[step][...]
    out[:, :ug] = stack[zone]
    out[:, ug : 2 * ug] = stack[zone ^ 1]
    out[:, 2 * ug : 2 * ug + qg] = stack[zone ^ 2][:, :qg]
    out[:, 2 * ug + qg :] = stack[zone ^ 3][:, : out.shape[1] - 2 * ug - qg]


def spread(place, parts, ref, span):
    core, chip = (place[0], place[1])
    piece = parts[0].shape[0]
    near = len(parts) // 2
    for step, part in enumerate(parts):
        seat = core if step < near else 1 - core
        ref[rows_at(seat * HALF + (chip ^ (step % near)) * piece, piece), :] = part[:, span].astype(
            F32
        )


def grad_kernel(count, place, *refs):
    parts = refs[:count]
    mq, mp, mu, md = refs[count : count + 4]
    gq, gp, gu, gd, nq, np_, nu, nd, flip = refs[count + 4 :]
    ug, qg = (gu.shape[1], gq.shape[1])
    spread(place, parts, gu, slice(0, ug))
    spread(place, parts, flip, slice(ug, 2 * ug))
    spread(place, parts, gq, slice(2 * ug, 2 * ug + qg))
    spread(place, parts, gp, slice(2 * ug + qg, None))
    gd[...] = flip[...].T
    nq[...] = muon_momentum * mq[...] + gq[...]
    np_[...] = muon_momentum * mp[...] + gp[...]
    nu[...] = muon_momentum * mu[...] + gu[...]
    nd[...] = muon_momentum * md[...] + gd[...]


def weight_kernel(count, place, *refs):
    parts = refs[:count]
    wq, wp, wu, wd = refs[count : count + 4]
    nq, np_, nu, nd, flip = refs[count + 4 :]
    ug, qg = (nu.shape[1], nq.shape[1])
    spread(place, parts, nu, slice(0, ug))
    spread(place, parts, flip, slice(ug, 2 * ug))
    spread(place, parts, nq, slice(2 * ug, 2 * ug + qg))
    spread(place, parts, np_, slice(2 * ug + qg, None))
    for new, old, factor in (
        (nq, wq, math.sqrt(3.0)),
        (np_, wp, 1.0),
        (nu, wu, math.sqrt(max(1.0, FF / D))),
    ):
        new[...] = old[...] - muon_rate * (factor * new[...] + muon_decay * old[...])
    nd[...] = wd[...] - muon_rate * (flip[...].T + muon_decay * wd[...])


CELL = 64
AREA = WIN * WIN
CELLS = (SIDE // WIN) ** 2
FOUR = 4


def flat(left, right):
    return lax.dot_general(left, right, (((1,), (1,)), ((), ())), preferred_element_type=F32)


def tall(left, right):
    return lax.dot_general(left, right, (((0,), (0,)), ((), ())), preferred_element_type=F32)


def segment_sum(value, ones):
    high, low = split(value)
    return dot32(high, ones) + dot32(low, ones)


def place_rows(source, target, index, scratch, order, factor=None):
    tokens = source.shape[1]
    scratch[...] = jnp.zeros_like(scratch)
    value = source[index]
    scratch[:tokens, :] = value if factor is None else (value.astype(F32) * factor).astype(BF)
    size = order.shape[0]
    moved = dot32(order[...], scratch[...])
    target[index * size : (index + 1) * size, :] = moved.astype(target.dtype)


def attend_kernel(
    head_width,
    place,
    images,
    wq,
    wp,
    vectors,
    bias,
    order,
    heads,
    ones,
    resid,
    qkv,
    mixed,
    probs,
    normed,
    scaled,
    inverse,
    scratch,
):
    slots = images.shape[0]
    size = CELLS * CELL
    scale = head_width ** (-0.5)
    for slot in range(slots):
        place_rows(images, resid, slot, scratch, order)
    shift = jnp.concatenate([vectors[2:3, :], jnp.zeros((1, D), F32), vectors[3:4, :]], 1)

    def project(slot, carry):
        rows = rows_at(slot * size, size)
        hat, back = standard(resid[rows, :])
        scaled[rows, :] = hat
        inverse[rows, :] = jnp.broadcast_to(back, (size, inverse.shape[1]))
        value = (hat * vectors[0:1, :] + vectors[1:2, :]).astype(BF)
        normed[rows, :] = value
        seen = lax.broadcasted_iota(jnp.int32, (size, 1), 0) % CELL < AREA
        full = dot32(value, wq[...]) + shift
        qkv[rows, :] = jnp.where(seen, full, 0.0).astype(BF)
        return carry

    lax.fori_loop(0, slots, project, 0)

    def window(cell, carry):
        rows = rows_at(cell * CELL, CELL)
        for part in range(D // 128):
            lanes = slice(part * 128, part * 128 + 128)
            wide = slice(part * 256, part * 256 + 256)
            query = qkv[rows, lanes]
            key = qkv[rows, D + part * 128 : D + part * 128 + 128]
            value = qkv[rows, 2 * D + part * 128 : 2 * D + part * 128 + 128]
            keys = jnp.concatenate([key] * FOUR, 0) * heads[...]
            values = jnp.concatenate([value] * FOUR, 0) * heads[...]
            scores = flat(query, keys) * scale + bias[cell % CELLS, :, wide]
            total = segment_sum(jnp.exp(scores), ones[...])
            chance = jnp.exp(scores - jnp.log(total))
            probs[rows, wide] = chance
            mixed[rows, lanes] = dot32(chance.astype(BF), values).astype(BF)
        return carry

    lax.fori_loop(0, slots * CELLS, window, 0)

    def finish(slot, carry):
        rows = rows_at(slot * size, size)
        resid[rows, :] = resid[rows, :] + dot32(mixed[rows, :], wp[...]) + vectors[4:5, :]
        return carry

    lax.fori_loop(0, slots, finish, 0)


def standard(value):
    centred = value - jnp.mean(value, -1, keepdims=True)
    back = lax.rsqrt(jnp.mean(centred * centred, -1, keepdims=True) + norm_eps)
    return (centred * back, back)


def hidden_kernel(
    ug,
    place,
    resid,
    grads,
    wu,
    wd,
    vectors,
    bias,
    order,
    output,
    keep,
    send,
    resid_back,
    sums,
    bias_grad,
    scratch,
    upstream,
    normed,
    turned,
    raised,
    total,
    back,
    hidden,
    slanted,
):
    slots, tokens = (grads.shape[0], grads.shape[1])
    size = order.shape[0]
    core, count = (place[0], place[4])
    for slot in range(slots):
        factor = jnp.where(slot < count, 1.0, 0.0)
        place_rows(grads, upstream, slot, scratch, order, factor)
    for slot in range(slots):
        rows = slice(slot * size, (slot + 1) * size)
        hat, _ = standard(resid[rows, :])
        normed[rows, :] = (hat * vectors[5:6, :] + vectors[6:7, :]).astype(BF)
    turned[...] = normed[...].T
    raised[...] = upstream[...].T
    total[...] = jnp.zeros_like(total)
    back[...] = jnp.zeros_like(back)
    blend = math.sqrt(2.0 / math.pi)
    near, away = (rows_at(core * HALF, HALF), rows_at((1 - core) * HALF, HALF))

    def chunk(index, carry):
        lanes = rows_at(index * ug, ug)
        gain = jnp.zeros((1, ug), F32)
        for slot in range(slots):
            rows = slice(slot * size, (slot + 1) * size)
            inner = dot32(normed[rows, :], wu[:, lanes]) + bias[:, lanes]
            cube = inner * inner
            tangent = jnp.tanh(blend * (inner + 0.044715 * inner * cube))
            hidden[rows, :] = (0.5 * inner * (1.0 + tangent)).astype(BF)
            slope = 0.5 * (1.0 + tangent) + 0.5 * inner * (1.0 - tangent * tangent) * blend * (
                1.0 + 3.0 * 0.044715 * cube
            )
            grad = dot32(upstream[rows, :], wd[:, lanes]) * slope
            gain = gain + jnp.sum(grad, 0, keepdims=True)
            slanted[rows, :] = grad.astype(BF)
        bias_grad[:, lanes] = gain
        total[...] += flat(hidden[...], wd[:, lanes])
        back[...] += flat(slanted[...], wu[:, lanes])
        first = rows_at(index * 2 * ug, ug)
        second = pl.ds(pl.multiple_of(index * 2 * ug + ug, ug), ug)
        keep[:, first] = dot32(turned[near, :], slanted[...]).astype(BF)
        send[:, first] = dot32(turned[away, :], slanted[...]).astype(BF)
        keep[:, second] = dot32(raised[near, :], hidden[...]).astype(BF)
        send[:, second] = dot32(raised[away, :], hidden[...]).astype(BF)
        return carry

    lax.fori_loop(0, wu.shape[1] // ug, chunk, 0)
    sums[...] = jnp.zeros_like(sums)
    for slot in range(slots):
        rows = slice(slot * size, (slot + 1) * size)
        final = resid[rows, :] + total[rows, :] + vectors[7:8, :]
        final = (final * jnp.where(slot < count, 1.0, 0.0)).astype(BF)
        output[slot] = tall(order[...], final)[:tokens, :].astype(BF)
        hat, inverse = standard(resid[rows, :])
        given = upstream[rows, :].astype(F32)
        value = back[rows, :]
        result = given + norm_back(value * vectors[5:6, :], hat, inverse)
        resid_back[rows, :] = result
        sums[0:1, :] += jnp.sum(result, 0, keepdims=True)
        sums[1:2, :] += jnp.sum(value * hat, 0, keepdims=True)
        sums[2:3, :] += jnp.sum(value, 0, keepdims=True)
        sums[3:4, :] += jnp.sum(given, 0, keepdims=True)


def scatter_columns(ref, value, groups, offset, width):
    stride = ref.shape[1] // groups
    for group in range(groups):
        start = group * stride + offset
        ref[:, start : start + width] = value[:, group * width : (group + 1) * width]


def scores_kernel(
    head_width,
    groups,
    place,
    resid_back,
    wp,
    qkv,
    mixed,
    probs,
    normed,
    heads,
    ones,
    keep,
    send,
    grads,
    sums,
    table,
    rounded,
    mixed_back,
    turned,
):
    core = place[0]
    near, away = (rows_at(core * HALF, HALF), rows_at((1 - core) * HALF, HALF))
    scale = head_width ** (-0.5)
    cells = qkv.shape[0] // CELL
    qg = 3 * D // groups
    rounded[...] = resid_back[...].astype(BF)
    mixed_back[...] = flat(rounded[...], wp[...]).astype(BF)
    turned[...] = mixed[...].T
    for out, half in ((keep, near), (send, away)):
        value = dot32(turned[half, :], rounded[...]).astype(BF)
        scatter_columns(out, value, groups, qg, D // groups)
    table[...] = jnp.zeros_like(table)
    sums[...] = jnp.zeros_like(sums)

    def window(cell, carry):
        rows = rows_at(cell * CELL, CELL)
        for part in range(D // 128):
            lanes = slice(part * 128, part * 128 + 128)
            wide = slice(part * 256, part * 256 + 256)
            query = qkv[rows, lanes]
            key = qkv[rows, D + part * 128 : D + part * 128 + 128]
            value = qkv[rows, 2 * D + part * 128 : 2 * D + part * 128 + 128]
            given = mixed_back[rows, lanes]
            mask = heads[...]
            keys = jnp.concatenate([key] * FOUR, 0) * mask
            values = jnp.concatenate([value] * FOUR, 0) * mask
            chance = probs[rows, wide]
            prob_back = flat(given, values)
            level = segment_sum(chance * prob_back, ones[...])
            score = chance * (prob_back - level)
            table[:, wide] += score
            score = score.astype(BF)
            query_back = dot32(score, keys) * scale
            loose = mask.astype(F32)

            def fold(value):
                value = value * loose
                parts = [value[item * CELL : (item + 1) * CELL, :] for item in range(FOUR)]
                return (parts[0] + parts[1]) + (parts[2] + parts[3])

            key_back = fold(tall(score, query)) * scale
            value_back = fold(tall(chance.astype(BF), given))
            sums[0:1, lanes] += jnp.sum(query_back, 0, keepdims=True)
            sums[1:2, lanes] += jnp.sum(value_back, 0, keepdims=True)
            grads[rows, lanes] = query_back.astype(BF)
            grads[rows, D + part * 128 : D + part * 128 + 128] = key_back.astype(BF)
            grads[rows, 2 * D + part * 128 : 2 * D + part * 128 + 128] = value_back.astype(BF)
        return carry

    lax.fori_loop(0, cells, window, 0)
    turned[...] = normed[...].T
    for out, half in ((keep, near), (send, away)):
        value = dot32(turned[half, :], grads[...]).astype(BF)
        scatter_columns(out, value, groups, 0, qg)


def input_kernel(
    place, resid_back, grads, wq, scaled, inverse, vectors, order, input_grad, sums
):
    slots, tokens = (input_grad.shape[0], input_grad.shape[1])
    size = order.shape[0]
    sums[...] = jnp.zeros_like(sums)
    for slot in range(slots):
        rows = slice(slot * size, (slot + 1) * size)
        value = flat(grads[rows, :], wq[...])
        hat = scaled[rows, :]
        sums[0:1, :] += jnp.sum(value * hat, 0, keepdims=True)
        sums[1:2, :] += jnp.sum(value, 0, keepdims=True)
        result = resid_back[rows, :] + norm_back(
            value * vectors[0:1, :], hat, inverse[rows, 0:1]
        )
        high, low = split(result)
        moved = tall(order[...], high) + tall(order[...], low)
        input_grad[slot] = moved[:tokens, :]


def block_tables(heads):
    line = np.arange(SIDE)
    rolled = (line - SHIFT) % SIDE
    row, column = (np.repeat(rolled, SIDE), np.tile(rolled, SIDE))
    cell = (row // WIN) * (SIDE // WIN) + column // WIN
    spot = cell * CELL + (row % WIN) * WIN + column % WIN
    order = np.zeros((CELLS * CELL, CELLS * CELL), np.float32)
    order[spot, np.arange(SIDE * SIDE)] = 1.0
    masks = np.repeat(np.arange(FOUR), CELL)[:, None] == np.arange(128)[None, :] // (D // heads)
    spans = np.arange(FOUR * CELL) // CELL
    ones = spans[:, None] == spans[None, :]
    return tuple((jnp.asarray(item, BF) for item in (order, masks, ones)))


def position_tables(rel_table, onehot, blocked):
    heads = rel_table.shape[1]
    bias = jnp.dot(onehot, rel_table, precision=lax.Precision.HIGHEST)
    bias = bias.reshape(AREA, AREA, heads).transpose(0, 2, 1)[None] + blocked[:, :, None, :]
    bias = jnp.pad(bias, ((0, 0), (0, 0), (0, 0), (0, CELL - AREA)), constant_values=-1e30)
    bias = jnp.pad(bias, ((0, 0), (0, CELL - AREA), (0, 0), (0, 0)))
    inside = np.arange(CELL) < AREA
    edge = np.where(inside[:, None] | inside[None, :], 0.0, -1e30).astype(np.float32)
    bias = bias + jnp.asarray(edge)[None, :, None, :]
    return bias.reshape(CELLS, CELL, heads * CELL)


def table_sums(summed, onehot, heads):
    summed = summed.reshape(CELL, heads, CELL)[:AREA, :, :AREA].transpose(1, 0, 2)
    return jnp.dot(
        summed.reshape(heads, AREA * AREA), onehot, precision=lax.Precision.HIGHEST
    ).T


def adam(grad, param, first, second):
    first_new = beta_first * first + (1.0 - beta_first) * grad
    second_new = beta_second * second + (1.0 - beta_second) * grad * grad
    first_hat = first_new / (1.0 - beta_first**adam_count)
    second_hat = second_new / (1.0 - beta_second**adam_count)
    return (
        param - adam_rate * first_hat / (jnp.sqrt(second_hat) + adam_eps),
        first_new,
        second_new,
    )


def local(
    images,
    grad_output,
    live_count,
    qkv_weight,
    proj_weight,
    up_weight,
    down_weight,
    qkv_moment,
    proj_moment,
    up_moment,
    down_moment,
    vectors,
    hidden_bias,
    rel_table,
    vector_first,
    vector_second,
    bias_first,
    bias_second,
    table_first,
    table_second,
):
    onehot, blocked = window_tables(SIDE, WIN, SHIFT)
    groups, members = (lax.axis_size("group"), lax.axis_size("dp"))
    chips = members // 2
    piece = D // members
    seat, zone = (lax.axis_index("dp"), lax.axis_index("group"))
    place = jnp.stack([seat & 1, seat >> 1, zone, seat, live_count.reshape(())]).astype(jnp.int32)
    ug, qg, pg = (up_weight.shape[1], qkv_weight.shape[1], proj_weight.shape[1])

    def zshift(value, step):
        return lax.ppermute(value, "group", [(item, item ^ step) for item in range(groups)])

    def dshift(value, step):
        return lax.ppermute(value, "dp", [(item, item ^ step) for item in range(members)])

    shard_up, shard_qkv, part_up, part_qkv, moment_rows = run(
        prep_kernel,
        "prep",
        place,
        [
            qkv_weight,
            proj_weight,
            up_weight,
            down_weight,
            qkv_moment,
            proj_moment,
            up_moment,
            down_moment,
        ],
        [
            shape((D, 2 * ug), BF),
            shape((D, qg + pg), BF),
            shape((2 * PART, 2 * ug), BF),
            shape((2 * PART, qg + pg), BF),
            shape((piece, 2 * ug + qg + pg), F32),
        ],
        [pltpu.VMEM((D, ug), F32)],
    )

    def gather(shard, part, widths, name):
        far = [zshift(part, step) for step in range(1, groups)]
        across = dshift(jnp.concatenate([item[:PART] for item in far]), 2)
        along = dshift(jnp.concatenate([item[PART:] for item in far]), 4)
        mine = far + [across, along]
        theirs = [dshift(item, 1) for item in mine]
        fits = all((width % 128 == 0 for width in widths))
        kept = widths if fits else (sum(widths),)
        joined = run(
            functools.partial(join_kernel, groups, kept),
            name,
            place,
            [shard, *mine, *theirs],
            [shape((D, groups * width), BF) for width in kept],
        )
        if fits:
            return joined
        joined = joined[0].reshape(D, groups, -1)
        cut = widths[0]
        return [joined[:, :, :cut].reshape(D, -1), joined[:, :, cut:].reshape(D, -1)]

    full_qkv, full_proj = gather(shard_qkv, part_qkv, (qg, pg), "join_qkv")
    full_up, full_flip = gather(shard_up, part_up, (ug, ug), "join_up")
    heads = rel_table.shape[1]
    slots, tokens, _ = images.shape
    order, head_mask, ones = block_tables(heads)
    bias = position_tables(rel_table, onehot, blocked)
    size = CELLS * CELL
    rows = slots * size
    resid, qkv_rows, mixed, probs, normed, scaled, inverse = run(
        functools.partial(attend_kernel, D // heads),
        "attend",
        place,
        [images, full_qkv, full_proj, vectors, bias, order, head_mask, ones],
        [
            shape((rows, D), F32),
            shape((rows, 3 * D), BF),
            shape((rows, D), BF),
            shape((rows, heads * CELL), F32),
            shape((rows, D), BF),
            shape((rows, D), F32),
            shape((rows, 128), F32),
        ],
        [pltpu.VMEM((size, D), BF)],
    )
    output, keep_up, send_up, resid_back, sums_hidden, bias_sum = run(
        functools.partial(hidden_kernel, ug),
        "hidden",
        place,
        [resid, grad_output, full_up, full_flip, vectors, hidden_bias[None], order],
        [
            shape(images.shape, BF),
            shape((HALF, 2 * FF), BF),
            shape((HALF, 2 * FF), BF),
            shape((rows, D), F32),
            shape((4, D), F32),
            shape((1, FF), F32),
        ],
        [
            pltpu.VMEM((size, D), BF),
            pltpu.VMEM((rows, D), BF),
            pltpu.VMEM((rows, D), BF),
            pltpu.VMEM((D, rows), BF),
            pltpu.VMEM((D, rows), BF),
            pltpu.VMEM((rows, D), F32),
            pltpu.VMEM((rows, D), F32),
            pltpu.VMEM((rows, ug), BF),
            pltpu.VMEM((rows, ug), BF),
        ],
    )
    keep_qkv, send_qkv, qkv_back, sums_scores, table = run(
        functools.partial(scores_kernel, D // heads, groups),
        "scores",
        place,
        [resid_back, full_proj, qkv_rows, mixed, probs, normed, head_mask, ones],
        [
            shape((HALF, 4 * D), BF),
            shape((HALF, 4 * D), BF),
            shape((rows, 3 * D), BF),
            shape((2, D), F32),
            shape((CELL, heads * CELL), F32),
        ],
        [pltpu.VMEM((rows, D), BF), pltpu.VMEM((rows, D), BF), pltpu.VMEM((D, rows), BF)],
    )
    input_grad, sums_input = run(
        input_kernel,
        "inputs",
        place,
        [resid_back, qkv_back, full_qkv, scaled, inverse, vectors, order],
        [shape(images.shape, F32), shape((2, D), F32)],
    )
    local_vector = jnp.concatenate([sums_input, sums_scores, sums_hidden])
    local_bias = bias_sum[0]
    local_table = table_sums(table, onehot, heads)

    def reduce(keep, send, name):
        width = keep.shape[1]
        own, *sends = run(
            halve_kernel,
            "halve_" + name,
            place,
            [keep, dshift(send, 1)],
            [shape((piece, width), F32)] + [shape((piece, width), BF)] * (chips - 1),
        )
        came = [dshift(item, 2 * (step + 1)) for step, item in enumerate(sends)]
        width = width // groups
        own, *sends = run(
            functools.partial(plane_kernel, chips),
            "plane_" + name,
            place,
            [own, *came],
            [shape((piece, width), F32)] + [shape((piece, width), BF)] * (groups - 1),
        )
        return [own] + [zshift(item, step + 1) for step, item in enumerate(sends)]

    first = reduce(keep_up, send_up, "up")
    second = reduce(keep_qkv, send_qkv, "qkv")
    grad_piece, *outgoing = run(
        functools.partial(momentum_kernel, groups, qg),
        "momentum",
        place,
        [*first, *second, moment_rows],
        [shape((piece, 2 * ug + qg + pg), BF)] + [shape((piece, ug), BF)] * groups,
        [pltpu.VMEM((max(groups, 4), piece, ug), BF)],
    )

    def share(value):
        near = [value] + [dshift(value, 2 * step) for step in range(1, chips)]
        return near + [dshift(item, 1) for item in near]

    owned = [outgoing[0]] + [zshift(outgoing[step], step) for step in range(1, groups)]
    everyone = share(jnp.concatenate(owned, 1))
    results = run(
        functools.partial(newton_kernel, members),
        "newton",
        place,
        everyone,
        [shape((piece, ug), BF)] * groups,
        [
            pltpu.VMEM((D, groups * ug), BF),
            pltpu.VMEM((D, D), F32),
            pltpu.VMEM((piece, D), F32),
        ],
    )
    back = [results[0]] + [zshift(results[step], step) for step in range(1, groups)]
    (packed,) = run(
        functools.partial(pack_kernel, groups, qg),
        "pack",
        place,
        back,
        [shape((piece, 2 * ug + qg + pg), BF)],
        [pltpu.VMEM((groups, piece, ug), BF)],
    )
    mats = [(D, qg), (D, pg), (D, ug), (ug, D)]
    (
        qkv_grad,
        proj_grad,
        up_grad,
        down_grad,
        qkv_momentum,
        proj_momentum,
        up_momentum,
        down_momentum,
    ) = run(
        functools.partial(grad_kernel, members),
        "grads",
        place,
        [*share(grad_piece), qkv_moment, proj_moment, up_moment, down_moment],
        [shape(item, F32) for item in mats + mats],
        [pltpu.VMEM((D, ug), F32)],
    )
    new_qkv, new_proj, new_up, new_down = run(
        functools.partial(weight_kernel, members),
        "weights",
        place,
        [*share(packed), qkv_weight, proj_weight, up_weight, down_weight],
        [shape(item, F32) for item in mats],
        [pltpu.VMEM((D, ug), F32)],
    )
    small = jnp.concatenate(
        [local_vector.reshape(-1), local_bias.reshape(-1), local_table.reshape(-1)]
    )
    pad = -small.size % 1024
    total = jnp.pad(small, (0, pad)).reshape(-1, 128)
    step = 1
    while step < members:
        total = total + dshift(total, step)
        step *= 2
    step = 1
    while step < groups:
        total = total + zshift(total, step)
        step *= 2
    total = total.reshape(-1)
    ends = np.cumsum([local_vector.size, local_bias.size, local_table.size])
    vector_grad = total[: ends[0]].reshape(local_vector.shape)
    bias_grad = total[ends[0] : ends[1]].reshape(local_bias.shape)
    table_grad = total[ends[1] : ends[2]].reshape(local_table.shape)
    new_vectors, vector_mean, vector_square = adam(
        vector_grad, vectors, vector_first, vector_second
    )
    new_bias, bias_mean, bias_square = adam(bias_grad, hidden_bias, bias_first, bias_second)
    new_table, table_mean, table_square = adam(table_grad, rel_table, table_first, table_second)
    return (
        output,
        input_grad,
        qkv_grad,
        proj_grad,
        up_grad,
        down_grad,
        vector_grad,
        bias_grad,
        table_grad,
        new_qkv,
        new_proj,
        new_up,
        new_down,
        qkv_momentum,
        proj_momentum,
        up_momentum,
        down_momentum,
        new_vectors,
        new_bias,
        new_table,
        vector_mean,
        vector_square,
        bias_mean,
        bias_square,
        table_mean,
        table_square,
    )


def solution(mesh):
    placed = (
        P(("dp", "group"), None, None),
        P(("dp", "group"), None, None),
        P("dp", "group"),
        P(None, "group"),
        P(None, "group"),
        P(None, "group"),
        P("group", None),
        P(None, "group"),
        P(None, "group"),
        P(None, "group"),
        P("group", None),
        P(),
        P(),
        P(),
        P(),
        P(),
        P(),
        P(),
        P(),
        P(),
    )
    return jax.shard_map(
        local,
        mesh=mesh,
        in_specs=placed,
        out_specs=(
            P(("dp", "group"), None, None),
            P(("dp", "group"), None, None),
            P(None, "group"),
            P(None, "group"),
            P(None, "group"),
            P("group", None),
            P(),
            P(),
            P(),
            P(None, "group"),
            P(None, "group"),
            P(None, "group"),
            P("group", None),
            P(None, "group"),
            P(None, "group"),
            P(None, "group"),
            P("group", None),
            P(),
            P(),
            P(),
            P(),
            P(),
            P(),
            P(),
            P(),
            P(),
        ),
        check_vma=False,
    )
```

profile of v0, /device:TPU:0, one launch (start us, length us, event | category | flops | bytes accessed | tf_op | source)
XLA Modules:
  0.0 305.8 jit_solution(4533959276345825063)
XLA Ops:
  2.0 4.4 %prep.1 = (bf16[512,1024]{1,0:T(8,128)(2,1)}, bf16[512,512]{1,0:T(8,128)(2,1)}, bf16[128,1024]{1,0:T(8,128)(2,1)}, bf16[128,512]{1,0:T(8,128)(2,1)}, f32[64,1536]{1,0:T(8,128)}) custom-call(s32[5]{0:T(128)} %stack.19.place, f32[512,384]{1,0:T(8,128)} %refs_8_.3, f32[512,128]{1,0:T(8,128)} %refs_9_.3, f32[512,512]{1,0:T(8,128)} %refs_10_.3, ...), custom_call_target="tpu_custom_call" | custom-call | bytes 8650752 | tf_op jit(solution)/shard_map/prep/pallas_call | solution.py:77
  6.4 5.1 %collective-permute-start.2 = (bf16[128,512]{1,0:T(8,128)(2,1)}, bf16[128,512]{1,0:T(8,128)(2,1)S(1)}, u32[]{:S(2)}, u32[]{:S(2)}) collective-permute-start(bf16[128,512]{1,0:T(8,128)(2,1)} %get-tuple-element.93), channel_id=1, source_target_pairs={{0,3},{1,2},{2,1},{3,0},{4,7},{5,6},{6,5},{7,4},{8,11},{9,10},{10,... | collective-permute-start | bytes 393224 | tf_op jit(solution)/shard_map/ppermute | solution.py:676
  12.1 3.8 %collective-permute-start.12 = (bf16[128,1024]{1,0:T(8,128)(2,1)}, bf16[128,1024]{1,0:T(8,128)(2,1)S(1)}, u32[]{:S(2)}, u32[]{:S(2)}) collective-permute-start(bf16[128,1024]{1,0:T(8,128)(2,1)} %get-tuple-element.98), channel_id=1, source_target_pairs={{0,3},{1,2},{2,1},{3,0},{4,7},{5,6},{6,5},{7,4},{8,11},{9,10},{10,... | collective-permute-start | bytes 786440 | tf_op jit(solution)/shard_map/ppermute | solution.py:676
  16.1 6.2 %collective-permute-start.10 = (bf16[128,1024]{1,0:T(8,128)(2,1)}, bf16[128,1024]{1,0:T(8,128)(2,1)S(1)}, u32[]{:S(2)}, u32[]{:S(2)}) collective-permute-start(bf16[128,1024]{1,0:T(8,128)(2,1)} %get-tuple-element.98), channel_id=1, source_target_pairs={{0,1},{1,0},{2,3},{3,2},{4,5},{5,4},{6,7},{7,6},{8,9},{9,8},{10,11... | collective-permute-start | bytes 786440 | tf_op jit(solution)/shard_map/ppermute | solution.py:676
  22.3 12.6 %collective-permute-done.1.refs_2_ = bf16[128,512]{1,0:T(8,128)(2,1)S(1)} collective-permute-done((bf16[128,512]{1,0:T(8,128)(2,1)}, bf16[128,512]{1,0:T(8,128)(2,1)S(1)}, u32[]{:S(2)}, u32[]{:S(2)}) %collective-permute-start.1) | collective-permute-done | bytes 131104 | tf_op jit(solution)/shard_map/ppermute | solution.py:676
  37.3 8.0 %collective-permute-done.11.refs_2_ = bf16[128,1024]{1,0:T(8,128)(2,1)S(1)} collective-permute-done((bf16[128,1024]{1,0:T(8,128)(2,1)}, bf16[128,1024]{1,0:T(8,128)(2,1)S(1)}, u32[]{:S(2)}, u32[]{:S(2)}) %collective-permute-start.11) | collective-permute-done | bytes 262176 | tf_op jit(solution)/shard_map/ppermute | solution.py:676
  54.3 7.7 %collective-permute-done.4.refs_5_ = bf16[192,512]{1,0:T(8,128)(2,1)S(1)} collective-permute-done((bf16[192,512]{1,0:T(8,128)(2,1)}, bf16[192,512]{1,0:T(8,128)(2,1)S(1)}, u32[]{:S(2)}, u32[]{:S(2)}) %collective-permute-start.4) | collective-permute-done | bytes 196640 | tf_op jit(solution)/shard_map/ppermute | solution.py:679
  72.1 16.6 %attend.1 = (f32[512,512]{1,0:T(8,128)}, bf16[512,1536]{1,0:T(8,128)(2,1)}, bf16[512,512]{1,0:T(8,128)(2,1)}, f32[512,1024]{1,0:T(8,128)}, bf16[512,512]{1,0:T(8...) custom-call(s32[5]{0:T(128)} %stack.19.place, bf16[2,196,512]{2,1,0:T(8,128)(2,1)} %copy.72.images, ...), custom_call_target="tpu_custom_call" | custom-call | bytes 10969088 | tf_op jit(solution)/shard_map/attend/pallas_call | solution.py:77
  89.5 4.5 %join_up.1 = (bf16[512,2048]{1,0:T(8,128)(2,1)}, bf16[512,2048]{1,0:T(8,128)(2,1)}) custom-call(s32[5]{0:T(128)} %stack.19.place, bf16[512,1024]{1,0:T(8,128)(2,1)} %get-tuple-element.97.refs_0_, bf16[128,1024]{1,0:T(8,128)(2,1)} %copy-done.5, bf16[128,1024]{1,0:T(8,128)(2,1)} %copy-done.4, bf16[128,1024]{1,0:T(8,128)(2,1)} %copy-done.3, ...), custom_call_target="tpu_custom_call" | custom-call | bytes 8388608 | tf_op jit(solution)/shard_map/join_up/pallas_call | solution.py:77
  94.0 15.1 %hidden.1 = (bf16[2,196,512]{2,1,0:T(8,128)(2,1)}, bf16[256,4096]{1,0:T(8,128)(2,1)}, bf16[256,4096]{1,0:T(8,128)(2,1)}, f32[512,512]{1,0:T(8,128)}, f32[4,512]{1,0:T(4,128)}, /*index=5*/f32[1,2048]{1,0:T(1,128)}) custom-call(s32[5]{0:T(128)} %stack.19.place, f32[512,512]{1,0:T(8,128)} %get-tuple-element.96.resid, bf16[2,196,512]{2,1,0:T(8,128)(2,1)} %copy.73.grads, ...), custom_call_target="tpu_custom_call" | custom-call | bytes 11460608 | tf_op jit(solution)/shard_map/hidden/pallas_call | solution.py:77
  109.5 19.4 %scores.1 = (bf16[256,2048]{1,0:T(8,128)(2,1)}, bf16[256,2048]{1,0:T(8,128)(2,1)}, bf16[512,1536]{1,0:T(8,128)(2,1)}, f32[2,512]{1,0:T(2,128)}, f32[64,1024]{1,0:T(8,128)}) custom-call(s32[5]{0:T(128)} %stack.19.place, f32[512,512]{1,0:T(8,128)} %get-tuple-element.102.resid_back, bf16[512,512]{1,0:T(8,128)(2,1)} %get-tuple-element.95.wp, ...), custom_call_target="tpu_custom_call" | custom-call | bytes 10424320 | tf_op jit(solution)/shard_map/scores/pallas_call | solution.py:77
  136.0 5.4 %inputs.1 = (f32[2,196,512]{2,1,0:T(8,128)}, f32[2,512]{1,0:T(2,128)}) custom-call(s32[5]{0:T(128)} %stack.19.place, f32[512,512]{1,0:T(8,128)} %get-tuple-element.102.resid_back, bf16[512,1536]{1,0:T(8,128)(2,1)} %get-tuple-element.107.grads, bf16[512,1536]{1,0:T(8,128)(2,1)} %get-tuple-element.94.wq, f32[512,512]{1,0:T(8,128)} %get-tuple-element.108.scaled, ...), custom_call_target="tpu_custom_call" | custom-call | bytes 6459392 | tf_op jit(solution)/shard_map/inputs/pallas_call | solution.py:77
  141.5 4.1 %halve_up.1 = (f32[64,4096]{1,0:T(8,128)}, bf16[64,4096]{1,0:T(8,128)(2,1)}, bf16[64,4096]{1,0:T(8,128)(2,1)}, bf16[64,4096]{1,0:T(8,128)(2,1)}) custom-call(s32[5]{0:T(128)} %stack.19.place, bf16[256,4096]{1,0:T(8,128)(2,1)} %get-tuple-element.111.keep, bf16[256,4096]{1,0:T(8,128)(2,1)} %collective-permute-done.20.came), custom_call_target="tpu_custom_call" | custom-call | bytes 6815744 | tf_op jit(solution)/shard_map/halve_up/pallas_call | solution.py:77
  153.6 4.1 %fusion.15 = f32[169,16]{1,0:T(8,128)S(1)} fusion(f32[2401,169]{1,0:T(8,128)S(1)} %copy-done.1, f32[16,2401]{1,0:T(8,128)S(1)} %reshape.90), kind=kOutput, calls=%fused_computation.38 | convolution fusion | flops 77907648 | bytes 1787556 | tf_op jit(solution)/shard_map/dot_general | solution.py:628
  157.8 25.4 %collective-permute-done.29.refs_2_ = bf16[64,2048]{1,0:T(8,128)(2,1)S(1)} collective-permute-done((bf16[64,2048]{1,0:T(8,128)(2,1)}, bf16[64,2048]{1,0:T(8,128)(2,1)S(1)}, u32[]{:S(2)}, u32[]{:S(2)}) %collective-permute-start.29) | collective-permute-done | bytes 262176 | tf_op jit(solution)/shard_map/ppermute | solution.py:679
  200.8 5.6 %collective-permute-done.25.refs_2_ = bf16[64,1024]{1,0:T(8,128)(2,1)S(1)} collective-permute-done((bf16[64,1024]{1,0:T(8,128)(2,1)}, bf16[64,1024]{1,0:T(8,128)(2,1)S(1)}, u32[]{:S(2)}, u32[]{:S(2)}) %collective-permute-start.25) | collective-permute-done | bytes 131104 | tf_op jit(solution)/shard_map/ppermute | solution.py:676
  215.0 4.1 %collective-permute-done.47 = bf16[64,512]{1,0:T(8,128)(2,1)S(1)} collective-permute-done((bf16[64,512]{1,0:T(8,128)(2,1)}, bf16[64,512]{1,0:T(8,128)(2,1)S(1)}, u32[]{:S(2)}, u32[]{:S(2)}) %collective-permute-start.47) | collective-permute-done | bytes 65568 | tf_op jit(solution)/shard_map/ppermute | solution.py:676
  225.1 10.1 %collective-permute-done.43 = f32[72,128]{1,0:T(8,128)S(1)} collective-permute-done((f32[72,128]{1,0:T(8,128)S(1)}, f32[72,128]{1,0:T(8,128)S(1)}, u32[]{:S(2)}, u32[]{:S(2)}) %collective-permute-start.43) | collective-permute-done | bytes 36896 | tf_op jit(solution)/shard_map/ppermute | solution.py:679
  250.4 17.9 %newton.1 = (bf16[64,512]{1,0:T(8,128)(2,1)}, bf16[64,512]{1,0:T(8,128)(2,1)}, bf16[64,512]{1,0:T(8,128)(2,1)}, bf16[64,512]{1,0:T(8,128)(2,1)}) custom-call(s32[5]{0:T(128)} %stack.19.place, bf16[64,2048]{1,0:T(8,128)(2,1)} %copy-done.10, bf16[64,2048]{1,0:T(8,128)(2,1)} %copy-done.18, bf16[64,2048]{1,0:T(8,128)(2,1)} %copy-done.17, ...), custom_call_target="tpu_custom_call" | custom-call | bytes 2359296 | tf_op jit(solution)/shard_map/newton/pallas_call | solution.py:77
  273.6 4.4 %collective-permute-done.57.refs_2_ = bf16[64,512]{1,0:T(8,128)(2,1)S(1)} collective-permute-done((bf16[64,512]{1,0:T(8,128)(2,1)}, bf16[64,512]{1,0:T(8,128)(2,1)S(1)}, u32[]{:S(2)}, u32[]{:S(2)}) %collective-permute-start.57) | collective-permute-done | bytes 65568 | tf_op jit(solution)/shard_map/ppermute | solution.py:676
  285.8 3.4 %collective-permute-done.61.refs_3_ = bf16[64,1536]{1,0:T(8,128)(2,1)S(1)} collective-permute-done((bf16[64,1536]{1,0:T(8,128)(2,1)}, bf16[64,1536]{1,0:T(8,128)(2,1)S(1)}, u32[]{:S(2)}, u32[]{:S(2)}) %collective-permute-start.61) | collective-permute-done | bytes 196640 | tf_op jit(solution)/shard_map/ppermute | solution.py:679
  289.2 3.7 %collective-permute-done.60.refs_2_ = bf16[64,1536]{1,0:T(8,128)(2,1)S(1)} collective-permute-done((bf16[64,1536]{1,0:T(8,128)(2,1)}, bf16[64,1536]{1,0:T(8,128)(2,1)S(1)}, u32[]{:S(2)}, u32[]{:S(2)}) %collective-permute-start.60) | collective-permute-done | bytes 196640 | tf_op jit(solution)/shard_map/ppermute | solution.py:679
  294.8 5.5 %grads.2 = (f32[512,384]{1,0:T(8,128)}, f32[512,128]{1,0:T(8,128)}, f32[512,512]{1,0:T(8,128)}, f32[512,512]{1,0:T(8,128)}, f32[512,384]{1,0:T(8,128)}, /*index=...) custom-call(s32[5]{0:T(128)} %stack.19.place, bf16[64,1536]{1,0:T(8,128)(2,1)} %get-tuple-element.132.refs_0_, ...), custom_call_target="tpu_custom_call" | custom-call | bytes 11010048 | tf_op jit(solution)/shard_map/grads/pallas_call | solution.py:77
  301.2 4.6 %weights.1 = (f32[512,384]{1,0:T(8,128)}, f32[512,128]{1,0:T(8,128)}, f32[512,512]{1,0:T(8,128)}, f32[512,512]{1,0:T(8,128)}) custom-call(s32[5]{0:T(128)} %stack.19.place, bf16[64,1536]{1,0:T(8,128)(2,1)} %pack.1.refs_0_, bf16[64,1536]{1,0:T(8,128)(2,1)} %copy-done.32, bf16[64,1536]{1,0:T(8,128)(2,1)} %copy-done.30, bf16[64,1536]{1,0:T(8,128)(2,1)} %copy-done.29, ...), custom_call_target="tpu_custom_call" | custom-call | bytes 7864320 | tf_op jit(solution)/shard_map/weights/pallas_call | solution.py:77
  (293 shorter events, 102.0 us)
Async XLA Ops:
  11.5 23.5 %collective-permute-start.1 = (bf16[128,512]{1,0:T(8,128)(2,1)}, bf16[128,512]{1,0:T(8,128)(2,1)S(1)}, u32[]{:S(2)}, u32[]{:S(2)}) collective-permute-start(bf16[128,512]{1,0:T(8,128)(2,1)} %get-tuple-element.93), channel_id=1, source_target_pairs={{0,2},{1,3},{2,0},{3,1},{4,6},{5,7},{6,4},{7,5},{8,10},{9,11},{10,... | collective-permute-start | bytes 393224 | tf_op jit(solution)/shard_map/ppermute | solution.py:676
  11.5 23.5 %collective-permute-start = (bf16[128,512]{1,0:T(8,128)(2,1)}, bf16[128,512]{1,0:T(8,128)(2,1)S(1)}, u32[]{:S(2)}, u32[]{:S(2)}) collective-permute-start(bf16[128,512]{1,0:T(8,128)(2,1)} %get-tuple-element.93), channel_id=1, source_target_pairs={{0,1},{1,0},{2,3},{3,2},{4,5},{5,4},{6,7},{7,6},{8,9},{9,8},{10,11... | collective-permute-start | bytes 393224 | tf_op jit(solution)/shard_map/ppermute | solution.py:676
  12.1 25.1 %collective-permute-start.12 = (bf16[128,1024]{1,0:T(8,128)(2,1)}, bf16[128,1024]{1,0:T(8,128)(2,1)S(1)}, u32[]{:S(2)}, u32[]{:S(2)}) collective-permute-start(bf16[128,1024]{1,0:T(8,128)(2,1)} %get-tuple-element.98), channel_id=1, source_target_pairs={{0,3},{1,2},{2,1},{3,0},{4,7},{5,6},{6,5},{7,4},{8,11},{9,10},{10,... | collective-permute-start | bytes 786440 | tf_op jit(solution)/shard_map/ppermute | solution.py:676
  15.9 29.4 %collective-permute-start.11 = (bf16[128,1024]{1,0:T(8,128)(2,1)}, bf16[128,1024]{1,0:T(8,128)(2,1)S(1)}, u32[]{:S(2)}, u32[]{:S(2)}) collective-permute-start(bf16[128,1024]{1,0:T(8,128)(2,1)} %get-tuple-element.98), channel_id=1, source_target_pairs={{0,2},{1,3},{2,0},{3,1},{4,6},{5,7},{6,4},{7,5},{8,10},{9,11},{10,... | collective-permute-start | bytes 786440 | tf_op jit(solution)/shard_map/ppermute | solution.py:676
  16.1 29.1 %collective-permute-start.10 = (bf16[128,1024]{1,0:T(8,128)(2,1)}, bf16[128,1024]{1,0:T(8,128)(2,1)S(1)}, u32[]{:S(2)}, u32[]{:S(2)}) collective-permute-start(bf16[128,1024]{1,0:T(8,128)(2,1)} %get-tuple-element.98), channel_id=1, source_target_pairs={{0,1},{1,0},{2,3},{3,2},{4,5},{5,4},{6,7},{7,6},{8,9},{9,8},{10,11... | collective-permute-start | bytes 786440 | tf_op jit(solution)/shard_map/ppermute | solution.py:676
  35.7 18.5 %collective-permute-start.3 = (bf16[192,512]{1,0:T(8,128)(2,1)}, bf16[192,512]{1,0:T(8,128)(2,1)S(1)}, u32[]{:S(2)}, u32[]{:S(2)}) collective-permute-start(bf16[192,512]{1,0:T(8,128)(2,1)} %pad_maximum_fusion.2), channel_id=1, source_target_pairs={{0,8},{4,12},{8,0},{12,4},{16,24},{20,28},{24,16},{28,20},{1,9},{5... | collective-permute-start | bytes 589832 | tf_op jit(solution)/shard_map/ppermute | solution.py:679
  62.0 26.7 %collective-permute-start.18 = (bf16[192,1024]{1,0:T(8,128)(2,1)}, bf16[192,1024]{1,0:T(8,128)(2,1)}, u32[]{:S(2)}, u32[]{:S(2)}) collective-permute-start(bf16[192,1024]{1,0:T(8,128)(2,1)} %collective-permute-done.13.refs_4_), channel_id=1, source_target_pairs={{0,4},{4,0},{8,12},{12,8},{16,20},{20,16},{24,28},{28,24},{1,5},{5... | collective-permute-start | bytes 1179656 | tf_op jit(solution)/shard_map/ppermute | solution.py:679
  62.5 26.2 %collective-permute-start.19 = (bf16[192,1024]{1,0:T(8,128)(2,1)}, bf16[192,1024]{1,0:T(8,128)(2,1)}, u32[]{:S(2)}, u32[]{:S(2)}) collective-permute-start(bf16[192,1024]{1,0:T(8,128)(2,1)} %collective-permute-done.14.refs_5_), channel_id=1, source_target_pairs={{0,4},{4,0},{8,12},{12,8},{16,20},{20,16},{24,28},{28,24},{1,5},{5... | collective-permute-start | bytes 1179656 | tf_op jit(solution)/shard_map/ppermute | solution.py:679
  65.2 23.4 %collective-permute-start.17 = (bf16[128,1024]{1,0:T(8,128)(2,1)S(1)}, bf16[128,1024]{1,0:T(8,128)(2,1)S(1)}, u32[]{:S(2)}, u32[]{:S(2)}) collective-permute-start(bf16[128,1024]{1,0:T(8,128)(2,1)S(1)} %collective-permute-done.12.refs_3_), channel_id=1, source_target_pairs={{0,4},{4,0},{8,12},{12,8},{16,20},{20,16},{24,28},{28,24},{1,5},{5... | collective-permute-start | bytes 786440 | tf_op jit(solution)/shard_map/ppermute | solution.py:679
  65.8 22.9 %collective-permute-start.16 = (bf16[128,1024]{1,0:T(8,128)(2,1)S(1)}, bf16[128,1024]{1,0:T(8,128)(2,1)S(1)}, u32[]{:S(2)}, u32[]{:S(2)}) collective-permute-start(bf16[128,1024]{1,0:T(8,128)(2,1)S(1)} %collective-permute-done.11.refs_2_), channel_id=1, source_target_pairs={{0,4},{4,0},{8,12},{12,8},{16,20},{20,16},{24,28},{28,24},{1,5},{5... | collective-permute-start | bytes 786440 | tf_op jit(solution)/shard_map/ppermute | solution.py:679
  67.1 21.6 %collective-permute-start.15 = (bf16[128,1024]{1,0:T(8,128)(2,1)S(1)}, bf16[128,1024]{1,0:T(8,128)(2,1)}, u32[]{:S(2)}, u32[]{:S(2)}) collective-permute-start(bf16[128,1024]{1,0:T(8,128)(2,1)S(1)} %collective-permute-done.10.refs_1_), channel_id=1, source_target_pairs={{0,4},{4,0},{8,12},{12,8},{16,20},{20,16},{24,28},{28,24},{1,5},{5... | collective-permute-start | bytes 786440 | tf_op jit(solution)/shard_map/ppermute | solution.py:679
  109.0 32.4 %collective-permute-start.20 = (bf16[256,4096]{1,0:T(8,128)(2,1)}, bf16[256,4096]{1,0:T(8,128)(2,1)}, u32[]{:S(2)}, u32[]{:S(2)}) collective-permute-start(bf16[256,4096]{1,0:T(8,128)(2,1)} %get-tuple-element.112), channel_id=1, source_target_pairs={{0,4},{4,0},{8,12},{12,8},{16,20},{20,16},{24,28},{28,24},{1,5},{5... | collective-permute-start | bytes 6291464 | tf_op jit(solution)/shard_map/ppermute | solution.py:679
  145.6 40.4 %collective-permute-start.21 = (bf16[64,4096]{1,0:T(8,128)(2,1)}, bf16[64,4096]{1,0:T(8,128)(2,1)}, u32[]{:S(2)}, u32[]{:S(2)}) collective-permute-start(bf16[64,4096]{1,0:T(8,128)(2,1)} %get-tuple-element.114), channel_id=1, source_target_pairs={{0,8},{4,12},{8,0},{12,4},{16,24},{20,28},{24,16},{28,20},{1,9},{5... | collective-permute-start | bytes 1572872 | tf_op jit(solution)/shard_map/ppermute | solution.py:679
  147.1 41.9 %collective-permute-start.22 = (bf16[64,4096]{1,0:T(8,128)(2,1)}, bf16[64,4096]{1,0:T(8,128)(2,1)}, u32[]{:S(2)}, u32[]{:S(2)}) collective-permute-start(bf16[64,4096]{1,0:T(8,128)(2,1)} %get-tuple-element.115), channel_id=1, source_target_pairs={{0,16},{4,20},{8,24},{12,28},{16,0},{20,4},{24,8},{28,12},{1,17},{... | collective-permute-start | bytes 1572872 | tf_op jit(solution)/shard_map/ppermute | solution.py:679
  148.6 41.9 %collective-permute-start.23 = (bf16[64,4096]{1,0:T(8,128)(2,1)}, bf16[64,4096]{1,0:T(8,128)(2,1)}, u32[]{:S(2)}, u32[]{:S(2)}) collective-permute-start(bf16[64,4096]{1,0:T(8,128)(2,1)} %get-tuple-element.116), channel_id=1, source_target_pairs={{0,24},{4,28},{8,16},{12,20},{16,8},{20,12},{24,0},{28,4},{1,25},{... | collective-permute-start | bytes 1572872 | tf_op jit(solution)/shard_map/ppermute | solution.py:679
  150.6 32.6 %collective-permute-start.29 = (bf16[64,2048]{1,0:T(8,128)(2,1)}, bf16[64,2048]{1,0:T(8,128)(2,1)S(1)}, u32[]{:S(2)}, u32[]{:S(2)}) collective-permute-start(bf16[64,2048]{1,0:T(8,128)(2,1)} %get-tuple-element.125), channel_id=1, source_target_pairs={{0,16},{4,20},{8,24},{12,28},{16,0},{20,4},{24,8},{28,12},{1,17},{... | collective-permute-start | bytes 786440 | tf_op jit(solution)/shard_map/ppermute | solution.py:679
  152.2 31.0 %collective-permute-start.30 = (bf16[64,2048]{1,0:T(8,128)(2,1)}, bf16[64,2048]{1,0:T(8,128)(2,1)}, u32[]{:S(2)}, u32[]{:S(2)}) collective-permute-start(bf16[64,2048]{1,0:T(8,128)(2,1)} %get-tuple-element.126), channel_id=1, source_target_pairs={{0,24},{4,28},{8,16},{12,20},{16,8},{20,12},{24,0},{28,4},{1,25},{... | collective-permute-start | bytes 786440 | tf_op jit(solution)/shard_map/ppermute | solution.py:679
  198.2 24.5 %collective-permute-start.42 = (f32[72,128]{1,0:T(8,128)}, f32[72,128]{1,0:T(8,128)}, u32[]{:S(2)}, u32[]{:S(2)}) collective-permute-start(f32[72,128]{1,0:T(8,128)} %fusion.4), channel_id=1, source_target_pairs={{0,8},{4,12},{8,0},{12,4},{16,24},{20,28},{24,16},{28,20},{1,9},{5... | collective-permute-start | bytes 110600 | tf_op jit(solution)/shard_map/ppermute | solution.py:679
  219.1 26.4 %collective-permute-start.52 = (bf16[64,2048]{1,0:T(8,128)(2,1)S(1)}, bf16[64,2048]{1,0:T(8,128)(2,1)S(1)}, u32[]{:S(2)}, u32[]{:S(2)}) collective-permute-start(bf16[64,2048]{1,0:T(8,128)(2,1)S(1)} %constant_dynamic-update-slice_fusion.refs_0_), channel_id=1, source_target_pairs={{0,4},{4,0},{8,12},{12,8},{16,20},{20,16},{24,28},{28,24},{1,5},{5... | collective-permute-start | bytes 786440 | tf_op jit(solution)/shard_map/ppermute | solution.py:679
  219.2 17.3 %collective-permute-start.51 = (bf16[64,2048]{1,0:T(8,128)(2,1)S(1)}, bf16[64,2048]{1,0:T(8,128)(2,1)S(1)}, u32[]{:S(2)}, u32[]{:S(2)}) collective-permute-start(bf16[64,2048]{1,0:T(8,128)(2,1)S(1)} %constant_dynamic-update-slice_fusion.refs_0_), channel_id=1, source_target_pairs={{0,24},{4,28},{8,16},{12,20},{16,8},{20,12},{24,0},{28,4},{1,25},{... | collective-permute-start | bytes 786440 | tf_op jit(solution)/shard_map/ppermute | solution.py:679
  244.1 25.5 %collective-permute-start.36 = (bf16[64,1536]{1,0:T(8,128)(2,1)}, bf16[64,1536]{1,0:T(8,128)(2,1)}, u32[]{:S(2)}, u32[]{:S(2)}) collective-permute-start(bf16[64,1536]{1,0:T(8,128)(2,1)} %get-tuple-element.132.refs_0_), channel_id=1, source_target_pairs={{0,24},{4,28},{8,16},{12,20},{16,8},{20,12},{24,0},{28,4},{1,25},{... | collective-permute-start | bytes 589832 | tf_op jit(solution)/shard_map/ppermute | solution.py:679
  245.5 25.4 %collective-permute-start.35 = (bf16[64,1536]{1,0:T(8,128)(2,1)}, bf16[64,1536]{1,0:T(8,128)(2,1)}, u32[]{:S(2)}, u32[]{:S(2)}) collective-permute-start(bf16[64,1536]{1,0:T(8,128)(2,1)} %get-tuple-element.132.refs_0_), channel_id=1, source_target_pairs={{0,16},{4,20},{8,24},{12,28},{16,0},{20,4},{24,8},{28,12},{1,17},{... | collective-permute-start | bytes 589832 | tf_op jit(solution)/shard_map/ppermute | solution.py:679
  248.7 33.1 %collective-permute-start.37 = (bf16[64,1536]{1,0:T(8,128)(2,1)}, bf16[64,1536]{1,0:T(8,128)(2,1)S(1)}, u32[]{:S(2)}, u32[]{:S(2)}) collective-permute-start(bf16[64,1536]{1,0:T(8,128)(2,1)} %get-tuple-element.132.refs_0_), channel_id=1, source_target_pairs={{0,4},{4,0},{8,12},{12,8},{16,20},{20,16},{24,28},{28,24},{1,5},{5... | collective-permute-start | bytes 589832 | tf_op jit(solution)/shard_map/ppermute | solution.py:679
  248.8 33.8 %collective-permute-start.34 = (bf16[64,1536]{1,0:T(8,128)(2,1)}, bf16[64,1536]{1,0:T(8,128)(2,1)S(1)}, u32[]{:S(2)}, u32[]{:S(2)}) collective-permute-start(bf16[64,1536]{1,0:T(8,128)(2,1)} %get-tuple-element.132.refs_0_), channel_id=1, source_target_pairs={{0,8},{4,12},{8,0},{12,4},{16,24},{20,28},{24,16},{28,20},{1,9},{5... | collective-permute-start | bytes 589832 | tf_op jit(solution)/shard_map/ppermute | solution.py:679
  (103 other events, 1274.4 us)
where the time goes:
time: 306 us
  Pallas kernels  112 us (37%)
  waiting for transfers between devices  95.2 us (31%)
  starting transfers between devices  65.9 us (22%)
  local copies, waits for them, and re-layouts  15.8 us (5%)
  other arithmetic  8.2 us (3%)
  matrix products  6.28 us (2%)
    pallas_call x16, Pallas kernels, run(): pl.pallas_call(kernel, out_shape=list(outs), in_specs=[pl.BlockSpec(memor...  112 us
    ppermute x46, waiting for transfers between devices, dshift(): lax.ppermute(value, 'dp', [(item, item ^ step) for item in range(members)])  53.2 us
    ppermute x20, waiting for transfers between devices, zshift(): lax.ppermute(value, 'group', [(item, item ^ step) for item in range(group...  42.1 us
    ppermute x20, starting transfers between devices, zshift(): lax.ppermute(value, 'group', [(item, item ^ step) for item in range(group...  36.6 us
    ppermute x46, starting transfers between devices, dshift(): lax.ppermute(value, 'dp', [(item, item ^ step) for item in range(members)])  29.3 us
    unnamed x132, local copies, waits for them, and re-layouts  11.7 us
  transfers between devices with their start and end apart: 66, of which 15 were waited for; matrix products, arithmetic and copies ran while one was open for 8% of the time, Pallas kernels for 27%

commit v1 on v0

--- a/solution.py
+++ b/solution.py
@@ -33,15 +33,7 @@
 newton_third = 2.0315
 
 
-def window_tables(side, window, shift):
-    steps = np.arange(window)
-    row_pos = np.repeat(steps, window)
-    col_pos = np.tile(steps, window)
-    span = 2 * window - 1
-    offset = (row_pos[:, None] - row_pos[None, :] + window - 1) * span + (
-        col_pos[:, None] - col_pos[None, :] + window - 1
-    )
-    onehot = (offset.reshape(-1)[:, None] == np.arange(span * span)[None, :]).astype(np.float32)
+def blocked_pairs(side, window, shift):
     line = np.arange(side)
     label = (line >= side - window).astype(np.int64) + (line >= side - shift).astype(np.int64)
     region = 3 * label[:, None] + label[None, :]
@@ -51,8 +43,19 @@
         .transpose(0, 2, 1, 3)
         .reshape(per_side * per_side, window * window)
     )
-    blocked = np.where(region[:, :, None] != region[:, None, :], mask_fill, 0.0).astype(np.float32)
-    return (jnp.asarray(onehot), jnp.asarray(blocked))
+    return np.where(region[:, :, None] != region[:, None, :], mask_fill, 0.0).astype(np.float32)
+
+
+def adam(grad, param, first, second):
+    first_new = beta_first * first + (1.0 - beta_first) * grad
+    second_new = beta_second * second + (1.0 - beta_second) * grad * grad
+    first_hat = first_new / (1.0 - beta_first**adam_count)
+    second_hat = second_new / (1.0 - beta_second**adam_count)
+    return (
+        param - adam_rate * first_hat / (jnp.sqrt(second_hat) + adam_eps),
+        first_new,
+        second_new,
+    )
 
 
 def norm_back(grad_scaled, scaled, inverse):
@@ -71,68 +74,151 @@
     return jax.ShapeDtypeStruct(tuple(dims), kind)
 
 
-def run(kernel, name, places, args, outs, scratch=(), flops=0):
+def run(
+    kernel, name, place, args, outs, scratch=(), far=(), raw=(), sent=(), room=4
+):
+    far = tuple(far)
+    arrays = [*args, *outs]
+    moved = sum((int(np.prod(item.shape)) * item.dtype.itemsize for item in arrays))
+    held = sum(
+        (
+            int(np.prod(item.shape)) * jnp.dtype(item.dtype).itemsize
+            for item in scratch
+            if item.memory_space == pltpu.VMEM
+        )
+    )
     vmem = pl.BlockSpec(memory_space=pltpu.VMEM)
-    moved = sum((int(np.prod(item.shape)) * item.dtype.itemsize for item in [*args, *outs]))
+    hbm = pl.BlockSpec(memory_space=pltpu.HBM)
+    buffers = [pltpu.VMEM(args[item].shape, args[item].dtype) for item in far]
+    if far:
+        buffers.append(pltpu.SemaphoreType.DMA((len(far),)))
+
+    def body(seat, *refs):
+        ins, rest = (list(refs[: len(args)]), list(refs[len(args) :]))
+        if far:
+            local, rest = (rest[len(outs) : len(outs) + len(far) + 1], rest)
+            rest = rest[: len(outs)] + rest[len(outs) + len(far) + 1 :]
+            copies = [
+                pltpu.make_async_copy(ins[item], local[spot], local[-1].at[spot])
+                for spot, item in enumerate(far)
+            ]
+            for copy in copies:
+                copy.start()
+            for copy in copies:
+                copy.wait()
+            for spot, item in enumerate(far):
+                ins[item] = local[spot]
+        kernel(seat, *ins, *rest)
+
+    remote = set(far) | set(raw)
     return pl.pallas_call(
-        kernel,
+        body,
         out_shape=list(outs),
-        in_specs=[pl.BlockSpec(memory_space=pltpu.SMEM)] + [vmem] * len(args),
-        out_specs=[vmem] * len(outs),
-        scratch_shapes=list(scratch),
+        in_specs=[pl.BlockSpec(memory_space=pltpu.SMEM)]
+        + [hbm if item in remote else vmem for item in range(len(args))],
+        out_specs=[hbm if item in sent else vmem for item in range(len(outs))],
+        scratch_shapes=buffers + list(scratch),
         name=name,
-        cost_estimate=pl.CostEstimate(flops=flops, bytes_accessed=moved, transcendentals=0),
-        compiler_params=pltpu.CompilerParams(vmem_limit_bytes=62 * 1024 * 1024),
-    )(places, *args)
+        cost_estimate=pl.CostEstimate(flops=0, bytes_accessed=moved, transcendentals=0),
+        compiler_params=pltpu.CompilerParams(
+            vmem_limit_bytes=min(62 << 20, moved + held + (room << 20))
+        ),
+    )(place, *args)
+
+
+def after(value, *others):
+    return lax.optimization_barrier((value, *others))[0]
 
 
 def rows_at(start, size):
     return pl.ds(pl.multiple_of(start, size), size)
 
 
-def prep_kernel(place, wq, wp, wu, wd, mq, mp, mu, md, sa, sb, pa, pb, mom, flip):
-    ug, qg = (wu.shape[1], wq.shape[1])
-    core, chip = (place[0], place[1])
-    sb[:, :qg] = wq[...].astype(BF)
-    sb[:, qg:] = wp[...].astype(BF)
-    sa[:, :ug] = wu[...].astype(BF)
-    sa[:, ug:] = wd[...].T.astype(BF)
-    for half in range(2):
-        bit = (chip >> half) & 1
-        source = rows_at(half * HALF + (bit * 2 + core) * PART, PART)
-        pa[half * PART : (half + 1) * PART, :] = sa[source, :]
-        pb[half * PART : (half + 1) * PART, :] = sb[source, :]
+def cast_kernel(place, left, right, shard, part):
+    width = left.shape[1]
+    shard[:, :width] = left[...].astype(BF)
+    shard[:, width:] = right[...].astype(BF)
+    part[...] = shard[rows_at(place[0] * HALF + (place[1] & 3) * PART, PART), :]
+
+
+def turn_kernel(place, wu, wd, mq, mp, mu, md, shard, part, mom, flip):
+    ug, qg = (wu.shape[1], mq.shape[1])
+    shard[:, :ug] = wu[...].astype(BF)
+    shard[:, ug:] = wd[...].T.astype(BF)
+    part[...] = shard[rows_at(place[0] * HALF + (place[1] & 3) * PART, PART), :]
     flip[...] = md[...].T
     piece = mom.shape[0]
-    source = rows_at(core * HALF + chip * piece, piece)
+    source = rows_at(place[0] * HALF + place[1] * piece, piece)
     mom[:, :ug] = mu[source, :]
     mom[:, ug : 2 * ug] = flip[source, :]
     mom[:, 2 * ug : 2 * ug + qg] = mq[source, :]
     mom[:, 2 * ug + qg :] = mp[source, :]
 
 
-def join_kernel(group_count, widths, place, *refs):
-    core, chip, zone = (place[0], place[1], place[2])
-    far = group_count - 1
-    own = refs[0]
-    mine = refs[1 : 1 + far] + refs[1 + far : 3 + far]
-    theirs = refs[3 + far : 3 + 2 * far] + refs[3 + 2 * far : 5 + 2 * far]
-    outs = refs[5 + 2 * far :]
+def join_kernel(group_count, widths, place, own, *refs):
+    core, chip, zone = (place[0], place[1] & 3, place[2])
+    parts, outs = (refs[:8], refs[8:])
     offset = 0
     for out, width in zip(outs, widths):
         span = slice(offset, offset + width)
         out[:, rows_at(zone * width, width)] = own[:, span]
         for step in range(1, group_count):
             columns = rows_at((zone ^ step) * width, width)
-            for parts, seat in ((mine, core), (theirs, 1 - core)):
-                for half in range(2):
-                    bit = (chip >> half) & 1
-                    base = half * HALF
-                    near = parts[step - 1][half * PART : (half + 1) * PART, span]
-                    out[rows_at(base + (bit * 2 + seat) * PART, PART), columns] = near
-                    swap = parts[far + half][(step - 1) * PART : step * PART, span]
-                    out[rows_at(base + ((1 - bit) * 2 + seat) * PART, PART), columns] = swap
+            for index, part in enumerate(parts):
+                seat = core if index < 4 else 1 - core
+                rows = rows_at(seat * HALF + (chip ^ (index % 4)) * PART, PART)
+                out[rows, columns] = part[(step - 1) * PART : step * PART, span]
         offset += width
+
+
+def stack_kernel(axis, place, *refs):
+    parts, out, sems = (refs[:-2], refs[-2], refs[-1])
+    size = parts[0].shape[axis]
+    copies = []
+    for step, part in enumerate(parts):
+        span = pl.ds(step * size, size)
+        target = out.at[span, :] if axis == 0 else out.at[:, span]
+        copies.append(pltpu.make_async_copy(part, target, sems.at[step]))
+    for copy in copies:
+        copy.start()
+    for copy in copies:
+        copy.wait()
+
+
+def weight_copies(place, groups, widths, sources, targets, sems):
+    if len(sources) == len(targets):
+        return [
+            [pltpu.make_async_copy(source, target, sems.at[spot])]
+            for spot, (source, target) in enumerate(zip(sources, targets))
+        ]
+    core, chip, zone = (place[0], place[1] & 3, place[2])
+    own, parts = (sources[0], sources[1:])
+    result, offset, spot = ([], 0, 0)
+    for target, width in zip(targets, widths):
+        span = pl.ds(offset, width)
+        copies = [
+            pltpu.make_async_copy(
+                own.at[:, span], target.at[:, rows_at(zone * width, width)], sems.at[spot]
+            )
+        ]
+        spot += 1
+        for step in range(1, groups):
+            columns = rows_at((zone ^ step) * width, width)
+            for index, part in enumerate(parts):
+                seat = core if index < 4 else 1 - core
+                rows = rows_at(seat * HALF + (chip ^ (index % 4)) * PART, PART)
+                source = part.at[pl.ds((step - 1) * PART, PART), span]
+                copies.append(
+                    pltpu.make_async_copy(source, target.at[rows, columns], sems.at[spot])
+                )
+                spot += 1
+        result.append(copies)
+        offset += width
+    return result
+
+
+def add_kernel(place, left, right, out):
+    out[...] = left[...] + right[...]
 
 
 def halve_kernel(place, keep, came, own, *sends):
@@ -207,11 +293,17 @@
 
 
 def newton_kernel(count, place, *refs):
-    parts, outs = (refs[:count], refs[count:-3])
-    whole, gram, lead = refs[-3:]
+    parts, outs = (refs[:count], refs[count:-4])
+    whole, gram, lead, sems = refs[-4:]
     piece = parts[0].shape[0]
-    for step, item in enumerate(parts):
-        whole[step * piece : (step + 1) * piece, :] = item[...]
+    copies = [
+        pltpu.make_async_copy(item, whole.at[pl.ds(step * piece, piece), :], sems.at[step])
+        for step, item in enumerate(parts)
+    ]
+    for copy in copies:
+        copy.start()
+    for copy in copies:
+        copy.wait()
     matrix = whole[...]
     raw = lax.dot_general(matrix, matrix, (((1,), (1,)), ((), ())), preferred_element_type=F32)
     row = lax.broadcasted_iota(jnp.int32, raw.shape, 0)
@@ -269,38 +361,89 @@
         )
 
 
+def load(sources, targets, sems):
+    copies = [
+        pltpu.make_async_copy(source, target, sems.at[spot])
+        for spot, (source, target) in enumerate(zip(sources, targets))
+    ]
+    for copy in copies:
+        copy.start()
+    return copies
+
+
+def spans_of(ug, qg, pg):
+    return (
+        slice(0, ug),
+        slice(ug, 2 * ug),
+        slice(2 * ug, 2 * ug + qg),
+        slice(2 * ug + qg, 2 * ug + qg + pg),
+    )
+
+
 def grad_kernel(count, place, *refs):
-    parts = refs[:count]
-    mq, mp, mu, md = refs[count : count + 4]
-    gq, gp, gu, gd, nq, np_, nu, nd, flip = refs[count + 4 :]
-    ug, qg = (gu.shape[1], gq.shape[1])
-    spread(place, parts, gu, slice(0, ug))
-    spread(place, parts, flip, slice(ug, 2 * ug))
-    spread(place, parts, gq, slice(2 * ug, 2 * ug + qg))
-    spread(place, parts, gp, slice(2 * ug + qg, None))
-    gd[...] = flip[...].T
-    nq[...] = muon_momentum * mq[...] + gq[...]
-    np_[...] = muon_momentum * mp[...] + gp[...]
-    nu[...] = muon_momentum * mu[...] + gu[...]
-    nd[...] = muon_momentum * md[...] + gd[...]
+    sources, outs = (refs[: count + 4], refs[count + 4 : count + 12])
+    held, rest = (refs[count + 12 : 2 * count + 16], refs[2 * count + 16 :])
+    grads, news, flip, sems, out_sems = (rest[:4], rest[4:8], rest[8], rest[9], rest[10])
+    copies = load(sources, held, sems)
+    parts, moments = (held[:count], held[count:])
+    for copy in copies[:count]:
+        copy.wait()
+    ug, qg, pg = (moments[0].shape[1], moments[2].shape[1], moments[3].shape[1])
+    waits = []
+    for item, span in enumerate(spans_of(ug, qg, pg)):
+        copies[count + item].wait()
+        if item == 1:
+            spread(place, parts, flip, span)
+            grads[item][...] = flip[...].T
+        else:
+            spread(place, parts, grads[item], span)
+        news[item][...] = muon_momentum * moments[item][...] + grads[item][...]
+        for spot, source in ((2 * item, grads[item]), (2 * item + 1, news[item])):
+            copy = pltpu.make_async_copy(source, outs[spot], out_sems.at[spot])
+            copy.start()
+            waits.append(copy)
+    for copy in waits:
+        copy.wait()
 
 
 def weight_kernel(count, place, *refs):
-    parts = refs[:count]
-    wq, wp, wu, wd = refs[count : count + 4]
-    nq, np_, nu, nd, flip = refs[count + 4 :]
-    ug, qg = (nu.shape[1], nq.shape[1])
-    spread(place, parts, nu, slice(0, ug))
-    spread(place, parts, flip, slice(ug, 2 * ug))
-    spread(place, parts, nq, slice(2 * ug, 2 * ug + qg))
-    spread(place, parts, np_, slice(2 * ug + qg, None))
-    for new, old, factor in (
-        (nq, wq, math.sqrt(3.0)),
-        (np_, wp, 1.0),
-        (nu, wu, math.sqrt(max(1.0, FF / D))),
-    ):
-        new[...] = old[...] - muon_rate * (factor * new[...] + muon_decay * old[...])
-    nd[...] = wd[...] - muon_rate * (flip[...].T + muon_decay * wd[...])
+    sources, outs = (refs[: count + 4], refs[count + 4 : count + 8])
+    held, rest = (refs[count + 8 : 2 * count + 12], refs[2 * count + 12 :])
+    news, flip, sems, out_sems = (rest[:4], rest[4], rest[5], rest[6])
+    copies = load(sources, held, sems)
+    parts, olds = (held[:count], held[count:])
+    for copy in copies[:count]:
+        copy.wait()
+    ug, qg, pg = (olds[0].shape[1], olds[2].shape[1], olds[3].shape[1])
+    factors = (math.sqrt(max(1.0, FF / D)), 1.0, math.sqrt(3.0), 1.0)
+    waits = []
+    for item, span in enumerate(spans_of(ug, qg, pg)):
+        copies[count + item].wait()
+        spread(place, parts, flip if item == 1 else news[item], span)
+        ortho = flip[...].T if item == 1 else news[item][...]
+        old = olds[item][...]
+        news[item][...] = old - muon_rate * (factors[item] * ortho + muon_decay * old)
+        copy = pltpu.make_async_copy(news[item], outs[item], out_sems.at[item])
+        copy.start()
+        waits.append(copy)
+    for copy in waits:
+        copy.wait()
+
+
+def adam_kernel(place, left, right, *refs):
+    total = left[...] + right[...]
+    ins, outs = (refs[:9], refs[9:])
+    heads, offsets = ins[6].shape
+    grads = (
+        total[:8, :],
+        jnp.concatenate([total[8 + item : 9 + item, :] for item in range(FF // D)], 1),
+        total[12 : 12 + heads, :offsets],
+    )
+    for item, grad in enumerate(grads):
+        value, first, second = (ref[...] for ref in ins[3 * item : 3 * item + 3])
+        updated = adam(grad, value, first, second)
+        for out, result in zip(outs[4 * item : 4 * item + 4], (grad, *updated)):
+            out[...] = result
 
 
 CELL = 64
@@ -332,31 +475,20 @@
     target[index * size : (index + 1) * size, :] = moved.astype(target.dtype)
 
 
-def attend_kernel(
-    head_width,
-    place,
-    images,
-    wq,
-    wp,
-    vectors,
-    bias,
-    order,
-    heads,
-    ones,
-    resid,
-    qkv,
-    mixed,
-    probs,
-    normed,
-    scaled,
-    inverse,
-    scratch,
-):
+def attend_kernel(head_width, groups, widths, count, place, images, vectors, bias, *refs):
+    order, heads, ones = refs[:3]
+    sources, rest = (refs[3 : 3 + count], refs[3 + count :])
+    resid, qkv, mixed, probs, normed, scaled, inverse, wq, wp, scratch, sems = rest
     slots = images.shape[0]
     size = CELLS * CELL
     scale = head_width ** (-0.5)
+    first, second = weight_copies(place, groups, widths, sources, (wq, wp), sems)
+    for copy in first + second:
+        copy.start()
     for slot in range(slots):
         place_rows(images, resid, slot, scratch, order)
+    for copy in first:
+        copy.wait()
     shift = jnp.concatenate([vectors[2:3, :], jnp.zeros((1, D), F32), vectors[3:4, :]], 1)
 
     def project(slot, carry):
@@ -392,6 +524,9 @@
 
     lax.fori_loop(0, slots * CELLS, window, 0)
 
+    for copy in second:
+        copy.wait()
+
     def finish(slot, carry):
         rows = rows_at(slot * size, size)
         resid[rows, :] = resid[rows, :] + dot32(mixed[rows, :], wp[...]) + vectors[4:5, :]
@@ -406,32 +541,13 @@
     return (centred * back, back)
 
 
-def hidden_kernel(
-    ug,
-    place,
-    resid,
-    grads,
-    wu,
-    wd,
-    vectors,
-    bias,
-    order,
-    output,
-    keep,
-    send,
-    resid_back,
-    sums,
-    bias_grad,
-    scratch,
-    upstream,
-    normed,
-    turned,
-    raised,
-    total,
-    back,
-    hidden,
-    slanted,
-):
+def hidden_kernel(ug, groups, count, place, resid, grads, vectors, bias, order, *refs):
+    sources, rest = (refs[:count], refs[count:])
+    output, keep, send, resid_back, sums, bias_grad = rest[:6]
+    wu, wd, scratch, upstream, normed, turned, raised, total, back, hidden, slanted, sems = rest[6:]
+    first, second = weight_copies(place, groups, (ug, ug), sources, (wu, wd), sems)
+    for copy in first + second:
+        copy.start()
     slots, tokens = (grads.shape[0], grads.shape[1])
     size = order.shape[0]
     core, count = (place[0], place[4])
@@ -446,6 +562,8 @@
     raised[...] = upstream[...].T
     total[...] = jnp.zeros_like(total)
     back[...] = jnp.zeros_like(back)
+    for copy in first + second:
+        copy.wait()
     blend = math.sqrt(2.0 / math.pi)
     near, away = (rows_at(core * HALF, HALF), rows_at((1 - core) * HALF, HALF))
 
@@ -500,14 +618,23 @@
         ref[:, start : start + width] = value[:, group * width : (group + 1) * width]
 
 
+def proj_kernel(place, resid_back, wp, mixed, keep, send, mixed_back, rounded, turned):
+    core = place[0]
+    rounded[...] = resid_back[...].astype(BF)
+    mixed_back[...] = flat(rounded[...], wp[...]).astype(BF)
+    turned[...] = mixed[...].T
+    for out, half in ((keep, core), (send, 1 - core)):
+        out[...] = dot32(turned[rows_at(half * HALF, HALF), :], rounded[...]).astype(BF)
+
+
 def scores_kernel(
     head_width,
     groups,
     place,
-    resid_back,
-    wp,
+    mixed_back,
+    keep_proj,
+    send_proj,
     qkv,
-    mixed,
     probs,
     normed,
     heads,
@@ -517,8 +644,6 @@
     grads,
     sums,
     table,
-    rounded,
-    mixed_back,
     turned,
 ):
     core = place[0]
@@ -526,11 +651,7 @@
     scale = head_width ** (-0.5)
     cells = qkv.shape[0] // CELL
     qg = 3 * D // groups
-    rounded[...] = resid_back[...].astype(BF)
-    mixed_back[...] = flat(rounded[...], wp[...]).astype(BF)
-    turned[...] = mixed[...].T
-    for out, half in ((keep, near), (send, away)):
-        value = dot32(turned[half, :], rounded[...]).astype(BF)
+    for out, value in ((keep, keep_proj), (send, send_proj)):
         scatter_columns(out, value, groups, qg, D // groups)
     table[...] = jnp.zeros_like(table)
     sums[...] = jnp.zeros_like(sums)
@@ -577,24 +698,39 @@
         scatter_columns(out, value, groups, 0, qg)
 
 
-def input_kernel(
-    place, resid_back, grads, wq, scaled, inverse, vectors, order, input_grad, sums
-):
+def input_kernel(place, *refs):
+    resid_back, grads, wq, scaled, inverse, vectors, order, sums_scores, sums_hidden = refs[:9]
+    bias_sum, table, spots, groups, input_grad, small, stack = refs[9:]
     slots, tokens = (input_grad.shape[0], input_grad.shape[1])
     size = order.shape[0]
-    sums[...] = jnp.zeros_like(sums)
+    small[...] = jnp.zeros_like(small)
     for slot in range(slots):
         rows = slice(slot * size, (slot + 1) * size)
         value = flat(grads[rows, :], wq[...])
         hat = scaled[rows, :]
-        sums[0:1, :] += jnp.sum(value * hat, 0, keepdims=True)
-        sums[1:2, :] += jnp.sum(value, 0, keepdims=True)
+        small[0:1, :] += jnp.sum(value * hat, 0, keepdims=True)
+        small[1:2, :] += jnp.sum(value, 0, keepdims=True)
         result = resid_back[rows, :] + norm_back(
             value * vectors[0:1, :], hat, inverse[rows, 0:1]
         )
         high, low = split(result)
         moved = tall(order[...], high) + tall(order[...], low)
         input_grad[slot] = moved[:tokens, :]
+    small[2:4, :] = sums_scores[...]
+    small[4:8, :] = sums_hidden[...]
+    for item in range(FF // D):
+        small[8 + item : 9 + item, :] = bias_sum[:, item * D : (item + 1) * D]
+    heads = table.shape[1] // CELL
+    for head in range(heads):
+        stack[head * CELL : (head + 1) * CELL, :] = table[:, head * CELL : (head + 1) * CELL]
+    for head in range(heads):
+        high, low = split(stack[head * CELL : (head + 1) * CELL, :])
+        spread_out = dot32(high, spots[...]) + dot32(low, spots[...])
+        moved = pltpu.roll(spread_out, 0, 1, stride=1, stride_axis=0)
+        high, low = split(moved)
+        banded = dot32(groups[...], high) + dot32(groups[...], low)
+        moved = pltpu.roll(banded, 0, 1, stride=WIN - 1, stride_axis=0)
+        small[12 + head : 13 + head, : moved.shape[1]] = jnp.sum(moved, 0, keepdims=True)
 
 
 def block_tables(heads):
@@ -608,38 +744,64 @@
     masks = np.repeat(np.arange(FOUR), CELL)[:, None] == np.arange(128)[None, :] // (D // heads)
     spans = np.arange(FOUR * CELL) // CELL
     ones = spans[:, None] == spans[None, :]
-    return tuple((jnp.asarray(item, BF) for item in (order, masks, ones)))
-
-
-def position_tables(rel_table, onehot, blocked):
-    heads = rel_table.shape[1]
-    bias = jnp.dot(onehot, rel_table, precision=lax.Precision.HIGHEST)
-    bias = bias.reshape(AREA, AREA, heads).transpose(0, 2, 1)[None] + blocked[:, :, None, :]
-    bias = jnp.pad(bias, ((0, 0), (0, 0), (0, 0), (0, CELL - AREA)), constant_values=-1e30)
-    bias = jnp.pad(bias, ((0, 0), (0, CELL - AREA), (0, 0), (0, 0)))
+    step = np.arange(AREA)
+    spots = np.zeros((CELL, 256), np.float32)
+    reach = 2 * WIN - 1
+    spots[step, reach * (WIN - 1) + WIN - 1 - reach * (step // WIN) - step % WIN] = 1.0
+    bands = np.zeros((8, CELL), np.float32)
+    bands[step // WIN, step] = 1.0
+    return tuple((jnp.asarray(item, BF) for item in (order, masks, ones, spots, bands)))
+
+
+def exact(left, right):
+    high = left.astype(BF)
+    rest = left - high.astype(F32)
+    middle = rest.astype(BF)
+    low = (rest - middle.astype(F32)).astype(BF)
+    return dot32(high, right) + (dot32(middle, right) + dot32(low, right))
+
+
+def bias_kernel(place, table, reverse, bands, picks, masks, bias, padded):
+    heads, offsets = table.shape
+    padded[...] = jnp.zeros_like(padded)
+    padded[:, :offsets] = table[...]
+    turned = exact(padded[...], reverse[...])
+    for pair in range(heads // 2):
+        both = []
+        for head in (2 * pair, 2 * pair + 1):
+            line = jnp.broadcast_to(turned[head : head + 1, :], (8, turned.shape[1]))
+            line = pltpu.roll(line, 0, 1, stride=WIN - 1, stride_axis=0)
+            line = exact_left(bands[...], line)
+            line = pltpu.roll(line, 0, 1, stride=1, stride_axis=0)
+            both.append(exact(line, picks[...]))
+        value = jnp.concatenate(both, 1)
+        for cell in range(CELLS):
+            bias[cell, :, pair * 128 : pair * 128 + 128] = value + masks[cell]
+
+
+def exact_left(left, right):
+    high = right.astype(BF)
+    rest = right - high.astype(F32)
+    middle = rest.astype(BF)
+    low = (rest - middle.astype(F32)).astype(BF)
+    return tall(left, high) + (tall(left, middle) + tall(left, low))
+
+
+def position_tables(blocked):
+    reach = 2 * WIN - 1
+    step = np.arange(AREA)
+    spot = reach * (step // WIN) + step % WIN
+    reverse = np.zeros((256, 256), np.float32)
+    line = np.arange(reach * reach)
+    reverse[line, reach * reach - 1 - line] = 1.0
+    picks = np.zeros((256, CELL), np.float32)
+    picks[reach * (WIN - 1) + WIN - 1 + spot, step] = 1.0
     inside = np.arange(CELL) < AREA
-    edge = np.where(inside[:, None] | inside[None, :], 0.0, -1e30).astype(np.float32)
-    bias = bias + jnp.asarray(edge)[None, :, None, :]
-    return bias.reshape(CELLS, CELL, heads * CELL)
-
-
-def table_sums(summed, onehot, heads):
-    summed = summed.reshape(CELL, heads, CELL)[:AREA, :, :AREA].transpose(1, 0, 2)
-    return jnp.dot(
-        summed.reshape(heads, AREA * AREA), onehot, precision=lax.Precision.HIGHEST
-    ).T
-
-
-def adam(grad, param, first, second):
-    first_new = beta_first * first + (1.0 - beta_first) * grad
-    second_new = beta_second * second + (1.0 - beta_second) * grad * grad
-    first_hat = first_new / (1.0 - beta_first**adam_count)
-    second_hat = second_new / (1.0 - beta_second**adam_count)
-    return (
-        param - adam_rate * first_hat / (jnp.sqrt(second_hat) + adam_eps),
-        first_new,
-        second_new,
-    )
+    masks = np.zeros((CELLS, CELL, CELL), np.float32)
+    masks[:, :AREA, :AREA] = blocked
+    masks = masks + np.where(inside[None, :], 0.0, -1e30).astype(np.float32)
+    masks = np.concatenate([masks, masks], 2)
+    return (jnp.asarray(reverse, BF), jnp.asarray(picks, BF), jnp.asarray(masks))
 
 
 def local(
@@ -664,7 +826,6 @@
     table_first,
     table_second,
 ):
-    onehot, blocked = window_tables(SIDE, WIN, SHIFT)
     groups, members = (lax.axis_size("group"), lax.axis_size("dp"))
     chips = members // 2
     piece = D // members
@@ -678,64 +839,87 @@
     def dshift(value, step):
         return lax.ppermute(value, "dp", [(item, item ^ step) for item in range(members)])
 
-    shard_up, shard_qkv, part_up, part_qkv, moment_rows = run(
-        prep_kernel,
-        "prep",
+    shard_qkv, part_qkv = run(
+        cast_kernel,
+        "cast",
         place,
-        [
-            qkv_weight,
-            proj_weight,
-            up_weight,
-            down_weight,
-            qkv_moment,
-            proj_moment,
-            up_moment,
-            down_moment,
-        ],
+        [qkv_weight, proj_weight],
+        [shape((D, qg + pg), BF), shape((PART, qg + pg), BF)],
+        far=range(2),
+        room=62,
+    )
+    shard_up, part_up, moment_rows = run(
+        turn_kernel,
+        "turn",
+        after(place, part_qkv),
+        [up_weight, down_weight, qkv_moment, proj_moment, up_moment, down_moment],
         [
             shape((D, 2 * ug), BF),
-            shape((D, qg + pg), BF),
-            shape((2 * PART, 2 * ug), BF),
-            shape((2 * PART, qg + pg), BF),
+            shape((PART, 2 * ug), BF),
             shape((piece, 2 * ug + qg + pg), F32),
         ],
         [pltpu.VMEM((D, ug), F32)],
-    )
-
-    def gather(shard, part, widths, name):
-        far = [zshift(part, step) for step in range(1, groups)]
-        across = dshift(jnp.concatenate([item[:PART] for item in far]), 2)
-        along = dshift(jnp.concatenate([item[PART:] for item in far]), 4)
-        mine = far + [across, along]
-        theirs = [dshift(item, 1) for item in mine]
-        fits = all((width % 128 == 0 for width in widths))
-        kept = widths if fits else (sum(widths),)
-        joined = run(
-            functools.partial(join_kernel, groups, kept),
+        far=range(6),
+        room=62,
+    )
+
+    heads = rel_table.shape[1]
+    order, head_mask, ones, spots, bands = block_tables(heads)
+    reverse, picks, masks = position_tables(blocked_pairs(SIDE, WIN, SHIFT))
+    (bias,) = run(
+        bias_kernel,
+        "bias",
+        after(place, part_up),
+        [rel_table.T, reverse, bands, picks, masks],
+        [shape((CELLS, CELL, heads * CELL), F32)],
+        [pltpu.VMEM((heads, 256), F32)],
+        far=range(5),
+    )
+
+    def stack(parts, axis, name, order_by):
+        dims = list(parts[0].shape)
+        dims[axis] *= len(parts)
+        (result,) = run(
+            functools.partial(stack_kernel, axis),
             name,
+            after(place, *order_by),
+            parts,
+            [shape(dims, BF)],
+            [pltpu.SemaphoreType.DMA((len(parts),))],
+            raw=range(len(parts)),
+        )
+        return result
+
+    def fetch(part, name, *order_by):
+        return stack([zshift(part, step) for step in range(1, groups)], 0, name, order_by)
+
+    def gather(shard, far):
+        mine = [far] + [dshift(far, 2 * step) for step in range(1, 4)]
+        return [shard, *mine, *(dshift(item, 1) for item in mine)]
+
+    far_qkv = fetch(part_qkv, "far_qkv", bias)
+    far_up = fetch(after(part_up, far_qkv), "far_up")
+    pieces_qkv = gather(shard_qkv, far_qkv)
+    pieces_up = gather(shard_up, far_up)
+    if qg % 128 or pg % 128:
+        (joined,) = run(
+            functools.partial(join_kernel, groups, (qg + pg,)),
+            "join",
             place,
-            [shard, *mine, *theirs],
-            [shape((D, groups * width), BF) for width in kept],
+            pieces_qkv,
+            [shape((D, groups * (qg + pg)), BF)],
         )
-        if fits:
-            return joined
-        joined = joined[0].reshape(D, groups, -1)
-        cut = widths[0]
-        return [joined[:, :, :cut].reshape(D, -1), joined[:, :, cut:].reshape(D, -1)]
-
-    full_qkv, full_proj = gather(shard_qkv, part_qkv, (qg, pg), "join_qkv")
-    full_up, full_flip = gather(shard_up, part_up, (ug, ug), "join_up")
-    heads = rel_table.shape[1]
+        joined = joined.reshape(D, groups, -1)
+        pieces_qkv = [joined[:, :, :qg].reshape(D, -1), joined[:, :, qg:].reshape(D, -1)]
     slots, tokens, _ = images.shape
-    order, head_mask, ones = block_tables(heads)
-    bias = position_tables(rel_table, onehot, blocked)
     size = CELLS * CELL
     rows = slots * size
-    resid, qkv_rows, mixed, probs, normed, scaled, inverse = run(
-        functools.partial(attend_kernel, D // heads),
+    count = len(pieces_qkv)
+    resid, qkv_rows, mixed, probs, normed, scaled, inverse, full_qkv, full_proj = run(
+        functools.partial(attend_kernel, D // heads, groups, (qg, pg), count),
         "attend",
-        place,
-        [images, full_qkv, full_proj, vectors, bias, order, head_mask, ones],
+        after(place, far_up),
+        [images, vectors, bias, order, head_mask, ones, *pieces_qkv],
         [
             shape((rows, D), F32),
             shape((rows, 3 * D), BF),
@@ -744,14 +928,18 @@
             shape((rows, D), BF),
             shape((rows, D), F32),
             shape((rows, 128), F32),
+            shape((D, 3 * D), BF),
+            shape((D, D), BF),
         ],
-        [pltpu.VMEM((size, D), BF)],
+        [pltpu.VMEM((size, D), BF), pltpu.SemaphoreType.DMA((2 + 16 * (groups - 1),))],
+        far=range(6),
+        raw=range(6, 6 + count),
     )
     output, keep_up, send_up, resid_back, sums_hidden, bias_sum = run(
-        functools.partial(hidden_kernel, ug),
+        functools.partial(hidden_kernel, ug, groups, len(pieces_up)),
         "hidden",
         place,
-        [resid, grad_output, full_up, full_flip, vectors, hidden_bias[None], order],
+        [resid, grad_output, vectors, hidden_bias[None], order, *pieces_up],
         [
             shape(images.shape, BF),
             shape((HALF, 2 * FF), BF),
@@ -761,6 +949,8 @@
             shape((1, FF), F32),
         ],
         [
+            pltpu.VMEM((D, FF), BF),
+            pltpu.VMEM((D, FF), BF),
             pltpu.VMEM((size, D), BF),
             pltpu.VMEM((rows, D), BF),
             pltpu.VMEM((rows, D), BF),
@@ -770,13 +960,49 @@
             pltpu.VMEM((rows, D), F32),
             pltpu.VMEM((rows, ug), BF),
             pltpu.VMEM((rows, ug), BF),
+            pltpu.SemaphoreType.DMA((2 + 16 * (groups - 1),)),
         ],
-    )
+        far=range(1, 5),
+        raw=range(5, 5 + len(pieces_up)),
+    )
+    keep_proj, send_proj, mixed_back = run(
+        proj_kernel,
+        "proj",
+        place,
+        [resid_back, full_proj, mixed],
+        [shape((HALF, D), BF), shape((HALF, D), BF), shape((rows, D), BF)],
+        [pltpu.VMEM((rows, D), BF), pltpu.VMEM((D, rows), BF)],
+    )
+
+    def halve(keep, came, order_by, name):
+        width = keep.shape[1]
+        return run(
+            halve_kernel,
+            "halve_" + name,
+            after(place, order_by),
+            [keep, came],
+            [shape((piece, width), F32)] + [shape((piece, width), BF)] * (chips - 1),
+            far=(1,),
+        )
+
+    def plane(own, sends, order_by, name):
+        came = [dshift(item, 2 * (step + 1)) for step, item in enumerate(sends)]
+        width = own.shape[1] // groups
+        return run(
+            functools.partial(plane_kernel, chips),
+            "plane_" + name,
+            after(place, order_by),
+            [own, *came],
+            [shape((piece, width), F32)] + [shape((piece, width), BF)] * (groups - 1),
+            far=range(1, chips),
+        )
+
+    own_up, *sends_up = halve(keep_up, dshift(send_up, 1), mixed_back, "up")
     keep_qkv, send_qkv, qkv_back, sums_scores, table = run(
         functools.partial(scores_kernel, D // heads, groups),
         "scores",
-        place,
-        [resid_back, full_proj, qkv_rows, mixed, probs, normed, head_mask, ones],
+        after(place, own_up),
+        [mixed_back, keep_proj, send_proj, qkv_rows, probs, normed, head_mask, ones],
         [
             shape((HALF, 4 * D), BF),
             shape((HALF, 4 * D), BF),
@@ -784,126 +1010,159 @@
             shape((2, D), F32),
             shape((CELL, heads * CELL), F32),
         ],
-        [pltpu.VMEM((rows, D), BF), pltpu.VMEM((rows, D), BF), pltpu.VMEM((D, rows), BF)],
-    )
-    input_grad, sums_input = run(
+        [pltpu.VMEM((D, rows), BF)],
+        far=(6, 7),
+    )
+    own_qkv, *sends_qkv = halve(keep_qkv, dshift(send_qkv, 1), table, "qkv")
+    input_grad, small = run(
         input_kernel,
         "inputs",
-        place,
-        [resid_back, qkv_back, full_qkv, scaled, inverse, vectors, order],
-        [shape(images.shape, F32), shape((2, D), F32)],
-    )
-    local_vector = jnp.concatenate([sums_input, sums_scores, sums_hidden])
-    local_bias = bias_sum[0]
-    local_table = table_sums(table, onehot, heads)
-
-    def reduce(keep, send, name):
-        width = keep.shape[1]
-        own, *sends = run(
-            halve_kernel,
-            "halve_" + name,
-            place,
-            [keep, dshift(send, 1)],
-            [shape((piece, width), F32)] + [shape((piece, width), BF)] * (chips - 1),
-        )
-        came = [dshift(item, 2 * (step + 1)) for step, item in enumerate(sends)]
-        width = width // groups
-        own, *sends = run(
-            functools.partial(plane_kernel, chips),
-            "plane_" + name,
-            place,
-            [own, *came],
-            [shape((piece, width), F32)] + [shape((piece, width), BF)] * (groups - 1),
-        )
-        return [own] + [zshift(item, step + 1) for step, item in enumerate(sends)]
-
-    first = reduce(keep_up, send_up, "up")
-    second = reduce(keep_qkv, send_qkv, "qkv")
+        after(place, own_qkv),
+        [
+            resid_back,
+            qkv_back,
+            full_qkv,
+            scaled,
+            inverse,
+            vectors,
+            order,
+            sums_scores,
+            sums_hidden,
+            bias_sum,
+            table,
+            spots,
+            bands,
+        ],
+        [shape(images.shape, F32), shape((12 + heads, D), F32)],
+        [pltpu.VMEM((heads * CELL, CELL), F32)],
+        far=(5, 6, 11, 12),
+    )
+    def add(left, right):
+        outs = [shape(left.shape, F32)]
+        return run(add_kernel, "add", place, [left, right], outs, far=(0, 1))[0]
+
+    own_up, *sends_up = plane(own_up, sends_up, small, "up")
+    first = [own_up] + [zshift(item, step + 1) for step, item in enumerate(sends_up)]
+    rounds = [functools.partial(dshift, step=1 << bit) for bit in range(members.bit_length() - 1)]
+    rounds += [functools.partial(zshift, step=1 << bit) for bit in range(groups.bit_length() - 1)]
+    total = after(small, own_qkv)
+    for item in rounds[: len(rounds) - 4]:
+        total = add(total, item(total))
+    own_qkv, *sends_qkv = plane(own_qkv, sends_qkv, total, "qkv")
+    second = [own_qkv] + [zshift(item, step + 1) for step, item in enumerate(sends_qkv)]
+    total = add(total, rounds[-4](total))
     grad_piece, *outgoing = run(
         functools.partial(momentum_kernel, groups, qg),
         "momentum",
-        place,
+        after(place, total),
         [*first, *second, moment_rows],
         [shape((piece, 2 * ug + qg + pg), BF)] + [shape((piece, ug), BF)] * groups,
         [pltpu.VMEM((max(groups, 4), piece, ug), BF)],
+        far=[*range(1, groups), *range(groups + 1, 2 * groups + 1)],
     )
 
     def share(value):
         near = [value] + [dshift(value, 2 * step) for step in range(1, chips)]
         return near + [dshift(item, 1) for item in near]
 
+    total = add(total, rounds[-3](total))
     owned = [outgoing[0]] + [zshift(outgoing[step], step) for step in range(1, groups)]
-    everyone = share(jnp.concatenate(owned, 1))
+    rows_owned = stack(owned, 1, "owned", (total,))
+    everyone = share(rows_owned)
+    total = add(total, rounds[-2](total))
     results = run(
         functools.partial(newton_kernel, members),
         "newton",
-        place,
+        after(place, total),
         everyone,
         [shape((piece, ug), BF)] * groups,
         [
             pltpu.VMEM((D, groups * ug), BF),
             pltpu.VMEM((D, D), F32),
             pltpu.VMEM((piece, D), F32),
+            pltpu.SemaphoreType.DMA((members,)),
         ],
-    )
+        raw=range(members),
+        room=12,
+    )
+    came = rounds[-1](total)
     back = [results[0]] + [zshift(results[step], step) for step in range(1, groups)]
+    states = [
+        vectors,
+        vector_first,
+        vector_second,
+        *(item[None] for item in (hidden_bias, bias_first, bias_second)),
+        *(item.T for item in (rel_table, table_first, table_second)),
+    ]
+    adams = run(
+        adam_kernel,
+        "adam",
+        after(place, results[0]),
+        [total, came, *states],
+        [shape(states[3 * (item // 4)].shape, F32) for item in range(12)],
+        far=range(11),
+        room=62,
+    )
     (packed,) = run(
         functools.partial(pack_kernel, groups, qg),
         "pack",
-        place,
+        after(place, adams[0]),
         back,
         [shape((piece, 2 * ug + qg + pg), BF)],
         [pltpu.VMEM((groups, piece, ug), BF)],
-    )
-    mats = [(D, qg), (D, pg), (D, ug), (ug, D)]
+        far=range(groups),
+    )
+    wide = 2 * ug + qg + pg
+    mats = [(D, ug), (ug, D), (D, qg), (D, pg)]
+    buffers = [pltpu.VMEM((piece, wide), BF)] * members + [pltpu.VMEM(item, F32) for item in mats]
+    double = [item for item in mats for _ in range(2)]
     (
+        up_grad,
+        up_momentum,
+        down_grad,
+        down_momentum,
         qkv_grad,
+        qkv_momentum,
         proj_grad,
-        up_grad,
-        down_grad,
-        qkv_momentum,
         proj_momentum,
-        up_momentum,
-        down_momentum,
     ) = run(
         functools.partial(grad_kernel, members),
         "grads",
-        place,
-        [*share(grad_piece), qkv_moment, proj_moment, up_moment, down_moment],
-        [shape(item, F32) for item in mats + mats],
-        [pltpu.VMEM((D, ug), F32)],
-    )
-    new_qkv, new_proj, new_up, new_down = run(
+        after(place, packed),
+        [*share(after(grad_piece, results[0])), up_moment, down_moment, qkv_moment, proj_moment],
+        [shape(item, F32) for item in double],
+        [
+            *buffers,
+            *[pltpu.VMEM(item, F32) for item in mats + mats],
+            pltpu.VMEM((D, ug), F32),
+            pltpu.SemaphoreType.DMA((members + 4,)),
+            pltpu.SemaphoreType.DMA((8,)),
+        ],
+        raw=range(members + 4),
+        sent=range(8),
+        room=62,
+    )
+    new_up, new_down, new_qkv, new_proj = run(
         functools.partial(weight_kernel, members),
         "weights",
-        place,
-        [*share(packed), qkv_weight, proj_weight, up_weight, down_weight],
+        after(place, qkv_grad),
+        [*share(packed), up_weight, down_weight, qkv_weight, proj_weight],
         [shape(item, F32) for item in mats],
-        [pltpu.VMEM((D, ug), F32)],
-    )
-    small = jnp.concatenate(
-        [local_vector.reshape(-1), local_bias.reshape(-1), local_table.reshape(-1)]
-    )
-    pad = -small.size % 1024
-    total = jnp.pad(small, (0, pad)).reshape(-1, 128)
-    step = 1
-    while step < members:
-        total = total + dshift(total, step)
-        step *= 2
-    step = 1
-    while step < groups:
-        total = total + zshift(total, step)
-        step *= 2
-    total = total.reshape(-1)
-    ends = np.cumsum([local_vector.size, local_bias.size, local_table.size])
-    vector_grad = total[: ends[0]].reshape(local_vector.shape)
-    bias_grad = total[ends[0] : ends[1]].reshape(local_bias.shape)
-    table_grad = total[ends[1] : ends[2]].reshape(local_table.shape)
-    new_vectors, vector_mean, vector_square = adam(
-        vector_grad, vectors, vector_first, vector_second
-    )
-    new_bias, bias_mean, bias_square = adam(bias_grad, hidden_bias, bias_first, bias_second)
-    new_table, table_mean, table_square = adam(table_grad, rel_table, table_first, table_second)
+        [
+            *buffers,
+            *[pltpu.VMEM(item, F32) for item in mats],
+            pltpu.VMEM((D, ug), F32),
+            pltpu.SemaphoreType.DMA((members + 4,)),
+            pltpu.SemaphoreType.DMA((4,)),
+        ],
+        raw=range(members + 4),
+        sent=range(4),
+        room=62,
+    )
+    vector_grad, new_vectors, vector_mean, vector_square = adams[:4]
+    bias_grad, new_bias, bias_mean, bias_square = (item[0] for item in adams[4:8])
+    table_grad, new_table, table_mean, table_square = (item.T for item in adams[8:])
+    output, input_grad = (after(output, packed), after(input_grad, packed))
     return (
         output,
         input_grad,

time: 306 us -> 250 us (0.82)
  waiting for transfers between devices: 95.2 us -> 80.9 us
  local copies, waits for them, and re-layouts: 15.8 us -> 3.46 us
  Pallas kernels: 112 us -> 102 us
  other arithmetic: 8.2 us -> 0 us
  matrix products: 6.28 us -> 0 us
  starting transfers between devices: 65.9 us -> 61.4 us
    ppermute x20, waiting for transfers between devices: 42.1 us -> 19.2 us  [zshift(): lax.ppermute(value, 'group', [(item, item ^ step) for item in range(group...]
    pallas_call x16 -> x25, Pallas kernels: 112 us -> 102 us  [run(): pl.pallas_call(body, out_shape=list(outs), in_specs=[pl.BlockSpec(memory_...]
    unnamed x132 -> x52, local copies, waits for them, and re-layouts: 11.7 us -> 2.79 us
    ppermute x46, waiting for transfers between devices: 53.2 us -> 61.7 us  [dshift(): lax.ppermute(value, 'dp', [(item, item ^ step) for item in range(members)])]
    ppermute x20, starting transfers between devices: 36.6 us -> 29.5 us  [zshift(): lax.ppermute(value, 'group', [(item, item ^ step) for item in range(group...]
    dot_general x2 -> x0, matrix products: 6.28 us -> none  [the longest x1 4.09 us: table_sums(): jnp.dot(summed.reshape(heads, AREA * AREA), onehot, precision=lax.Precisi...]
    sub x3 -> x0, other arithmetic: 3.36 us -> none  [adam(): param - adam_rate * first_hat / (jnp.sqrt(second_hat) + adam_eps)]
    reshape x6 -> x0, local copies, waits for them, and re-layouts: 3.09 us -> none  [the longest x1 1.54 us: position_tables(): return bias.reshape(CELLS, CELL, heads * CELL)]
  transfers between devices with their start and end apart: 66 -> 66, of which waited for: 15 -> 21; matrix products, arithmetic and copies ran while one was open for 8% -> 1% of each run, Pallas kernels for 27% -> 25%
where the time goes in v1:
time: 250 us
  Pallas kernels  102 us (41%)
  waiting for transfers between devices  80.9 us (32%)
  starting transfers between devices  61.4 us (25%)
  local copies, waits for them, and re-layouts  3.46 us (1%)
    pallas_call x25, Pallas kernels, run(): pl.pallas_call(body, out_shape=list(outs), in_specs=[pl.BlockSpec(memory_...  102 us
    ppermute x46, waiting for transfers between devices, dshift(): lax.ppermute(value, 'dp', [(item, item ^ step) for item in range(members)])  61.7 us
    ppermute x46, starting transfers between devices, dshift(): lax.ppermute(value, 'dp', [(item, item ^ step) for item in range(members)])  31.9 us
    ppermute x20, starting transfers between devices, zshift(): lax.ppermute(value, 'group', [(item, item ^ step) for item in range(group...  29.5 us
    ppermute x20, waiting for transfers between devices, zshift(): lax.ppermute(value, 'group', [(item, item ^ step) for item in range(group...  19.2 us
  transfers between devices with their start and end apart: 66, of which 21 were waited for; matrix products, arithmetic and copies ran while one was open for 1% of the time, Pallas kernels for 25%

profile of v1, /device:TPU:0, one launch (start us, length us, event | category | flops | bytes accessed | tf_op | source)
XLA Modules:
  0.0 250.0 jit_solution(8969374850412557730)
XLA Ops:
  4.8 5.1 %collective-permute-start.2 = (bf16[64,512]{1,0:T(8,128)(2,1)}, bf16[64,512]{1,0:T(8,128)(2,1)S(1)}, u32[]{:S(2)}, u32[]{:S(2)}) collective-permute-start(bf16[64,512]{1,0:T(8,128)(2,1)} %get-tuple-element.127), channel_id=1, source_target_pairs={{0,3},{1,2},{2,1},{3,0},{4,7},{5,6},{6,5},{7,4},{8,11},{9,10},{10,... | collective-permute-start | bytes 196616 | tf_op jit(solution)/shard_map/ppermute | solution.py:837
  10.6 4.6 %turn.1 = (bf16[512,1024]{1,0:T(8,128)(2,1)}, bf16[64,1024]{1,0:T(8,128)(2,1)}, f32[64,1536]{1,0:T(8,128)}) custom-call(s32[5]{0:T(128)} %stack.19.seat, f32[512,512]{1,0:T(8,128)} %refs_8_.3, f32[512,512]{1,0:T(8,128)} %refs_9_.3, f32[512,384]{1,0:T(8,128)} %refs_10_.2, f32[512,128]{1,0:T(8,128)} %refs_11_.3, f32[512,512]{1,0:T(8,128)} %refs_8_.2, ...), custom_call_target="tpu_custom_call" | custom-call | bytes 6815744 | tf_op jit(solution)/shard_map/turn/pallas_call | solution.py:114
  15.3 3.0 %bias.1.refs_2_ = f32[4,64,1024]{2,1,0:T(8,128)S(1)} custom-call(s32[5]{0:T(128)S(1)} %copy-done.6, f32[16,169]{1,0:T(8,128)S(1)} %bitcast.21, bf16[256,256]{1,0:T(8,128)(2,1)S(1)} %copy-done.13, bf16[8,64]{1,0:T(8,128)(2,1)S(1)} %copy-done.18, bf16[256,64]{1,0:T(8,128)(2,1)S(1)} %copy-done.15, f32[4,64,128]{2,1,0:T(8,128)S(1)} %copy-done.12), custom_call_target="tpu_custom_call" | custom-call | bytes 1355328 | tf_op jit(solution)/shard_map/bias/pallas_call | solution.py:114
  19.2 3.8 %collective-permute-start.5 = (bf16[64,1024]{1,0:T(8,128)(2,1)}, bf16[64,1024]{1,0:T(8,128)(2,1)S(1)}, u32[]{:S(2)}, u32[]{:S(2)}) collective-permute-start(bf16[64,1024]{1,0:T(8,128)(2,1)} %get-tuple-element.132), channel_id=1, source_target_pairs={{0,3},{1,2},{2,1},{3,0},{4,7},{5,6},{6,5},{7,4},{8,11},{9,10},{10,... | collective-permute-start | bytes 393224 | tf_op jit(solution)/shard_map/ppermute | solution.py:837
  29.4 5.2 %collective-permute-done.4.refs_1_ = bf16[64,1024]{1,0:T(8,128)(2,1)S(1)} collective-permute-done((bf16[64,1024]{1,0:T(8,128)(2,1)}, bf16[64,1024]{1,0:T(8,128)(2,1)S(1)}, u32[]{:S(2)}, u32[]{:S(2)}) %collective-permute-start.4) | collective-permute-done | bytes 131104 | tf_op jit(solution)/shard_map/ppermute | solution.py:837
  40.7 19.2 %collective-permute-done.6.refs_8_ = bf16[192,512]{1,0:T(8,128)(2,1)S(1)} collective-permute-done((bf16[192,512]{1,0:T(8,128)(2,1)S(1)}, bf16[192,512]{1,0:T(8,128)(2,1)S(1)}, u32[]{:S(2)}, u32[]{:S(2)}) %collective-permute-start.6) | collective-permute-done | bytes 196640 | tf_op jit(solution)/shard_map/ppermute | solution.py:840
  64.0 14.3 %attend.1 = (f32[512,512]{1,0:T(8,128)S(1)}, bf16[512,1536]{1,0:T(8,128)(2,1)S(1)}, bf16[512,512]{1,0:T(8,128)(2,1)S(1)}, f32[512,1024]{1,0:T(8,128)S(1)}, bf16[...) custom-call(s32[5]{0:T(128)S(1)} %copy-done.6, ...), custom_call_target="tpu_custom_call" | custom-call | bytes 13066240 | tf_op jit(solution)/shard_map/attend/pallas_call | solution.py:114
  78.3 13.3 %hidden.1 = (bf16[2,196,512]{2,1,0:T(8,128)(2,1)S(1)}, bf16[256,4096]{1,0:T(8,128)(2,1)S(1)}, bf16[256,4096]{1,0:T(8,128)(2,1)S(1)}, f32[512,512]{1,0:T(8,128)S(...) custom-call(s32[5]{0:T(128)S(1)} %copy-done.6, f32[512,512]{1,0:T(8,128)S(1)} %get-tuple-element.135.refs_0_, ...), custom_call_target="tpu_custom_call" | custom-call | bytes 11460608 | tf_op jit(solution)/shard_map/hidden/pallas_call | solution.py:114
  97.0 15.3 %scores.1 = (bf16[256,2048]{1,0:T(8,128)(2,1)S(1)}, bf16[256,2048]{1,0:T(8,128)(2,1)S(1)}, bf16[512,1536]{1,0:T(8,128)(2,1)S(1)}, f32[2,512]{1,0:T(2,128)S(1)}, f32[64,1024]{1,0:T(8,128)S(1)}) custom-call(s32[5]{0:T(128)S(1)} %copy-done.6, bf16[512,512]{1,0:T(8,128)(2,1)S(1)} %get-tuple-element.141.refs_0_, bf16[256,512]{1,0:T(8,128)(2,1)S(1)} %get-tuple-element.147.refs_1_, ...), custom_call_target="tpu_custom_call" | custom-call | bytes 9375744 | tf_op jit(solution)/shard_map/scores/pallas_call | solution.py:114
  119.1 8.4 %collective-permute-done.26.refs_1_ = bf16[64,4096]{1,0:T(8,128)(2,1)S(1)} collective-permute-done((bf16[64,4096]{1,0:T(8,128)(2,1)S(1)}, bf16[64,4096]{1,0:T(8,128)(2,1)S(1)}, u32[]{:S(2)}, u32[]{:S(2)}) %collective-permute-start.26) | collective-permute-done | bytes 524320 | tf_op jit(solution)/shard_map/ppermute | solution.py:840
  128.9 6.8 %inputs.1 = (f32[2,196,512]{2,1,0:T(8,128)S(1)}, f32[28,512]{1,0:T(8,128)S(1)}) custom-call(s32[5]{0:T(128)S(1)} %copy-done.6, f32[512,512]{1,0:T(8,128)S(1)} %get-tuple-element.138.refs_0_, bf16[512,1536]{1,0:T(8,128)(2,1)S(1)} %get-tuple-element.158.refs_1_, bf16[512,1536]{1,0:T(8,128)(2,1)S(1)} %get-tuple-element.159.refs_2_, ...), custom_call_target="tpu_custom_call" | custom-call | bytes 6829056 | tf_op jit(solution)/shard_map/inputs/pallas_call | solution.py:114
  135.7 4.5 %collective-permute-done.27.refs_2_ = bf16[64,4096]{1,0:T(8,128)(2,1)S(1)} collective-permute-done((bf16[64,4096]{1,0:T(8,128)(2,1)S(1)}, bf16[64,4096]{1,0:T(8,128)(2,1)S(1)}, u32[]{:S(2)}, u32[]{:S(2)}) %collective-permute-start.27) | collective-permute-done | bytes 524320 | tf_op jit(solution)/shard_map/ppermute | solution.py:840
  142.6 2.8 %collective-permute-start.30 = (bf16[64,1024]{1,0:T(8,128)(2,1)S(1)}, bf16[64,1024]{1,0:T(8,128)(2,1)S(1)}, u32[]{:S(2)}, u32[]{:S(2)}) collective-permute-start(bf16[64,1024]{1,0:T(8,128)(2,1)S(1)} %get-tuple-element.176), channel_id=1, source_target_pairs={{0,2},{1,3},{2,0},{3,1},{4,6},{5,7},{6,4},{7,5},{8,10},{9,11},{10,... | collective-permute-start | bytes 393224 | tf_op jit(solution)/shard_map/ppermute | solution.py:837
  147.5 2.9 %collective-permute-done.33.refs_2_ = bf16[64,2048]{1,0:T(8,128)(2,1)S(1)} collective-permute-done((bf16[64,2048]{1,0:T(8,128)(2,1)S(1)}, bf16[64,2048]{1,0:T(8,128)(2,1)S(1)}, u32[]{:S(2)}, u32[]{:S(2)}) %collective-permute-start.33) | collective-permute-done | bytes 262176 | tf_op jit(solution)/shard_map/ppermute | solution.py:840
  151.8 2.9 %collective-permute-done.23.refs_1_ = f32[28,512]{1,0:T(8,128)S(1)} collective-permute-done((f32[28,512]{1,0:T(8,128)S(1)}, f32[28,512]{1,0:T(8,128)S(1)}, u32[]{:S(2)}, u32[]{:S(2)}) %collective-permute-start.23) | collective-permute-done | bytes 57376 | tf_op jit(solution)/shard_map/ppermute | solution.py:840
  158.0 4.5 %collective-permute-done.36.refs_6_ = bf16[64,512]{1,0:T(8,128)(2,1)S(1)} collective-permute-done((bf16[64,512]{1,0:T(8,128)(2,1)S(1)}, bf16[64,512]{1,0:T(8,128)(2,1)S(1)}, u32[]{:S(2)}, u32[]{:S(2)}) %collective-permute-start.36) | collective-permute-done | bytes 65568 | tf_op jit(solution)/shard_map/ppermute | solution.py:837
  169.3 3.8 %collective-permute-done.24.refs_1_ = f32[28,512]{1,0:T(8,128)S(1)} collective-permute-done((f32[28,512]{1,0:T(8,128)S(1)}, f32[28,512]{1,0:T(8,128)S(1)}, u32[]{:S(2)}, u32[]{:S(2)}) %collective-permute-start.24) | collective-permute-done | bytes 57376 | tf_op jit(solution)/shard_map/ppermute | solution.py:840
  178.0 5.9 %collective-permute-done.43.refs_3_ = bf16[64,2048]{1,0:T(8,128)(2,1)S(1)} collective-permute-done((bf16[64,2048]{1,0:T(8,128)(2,1)S(1)}, bf16[64,2048]{1,0:T(8,128)(2,1)S(1)}, u32[]{:S(2)}, u32[]{:S(2)}) %collective-permute-start.43) | collective-permute-done | bytes 262176 | tf_op jit(solution)/shard_map/ppermute | solution.py:840
  188.1 3.1 %collective-permute-done.25.refs_1_ = f32[28,512]{1,0:T(8,128)S(1)} collective-permute-done((f32[28,512]{1,0:T(8,128)S(1)}, f32[28,512]{1,0:T(8,128)S(1)}, u32[]{:S(2)}, u32[]{:S(2)}) %collective-permute-start.25) | collective-permute-done | bytes 57376 | tf_op jit(solution)/shard_map/ppermute | solution.py:837
  193.6 16.2 %newton.1 = (bf16[64,512]{1,0:T(8,128)(2,1)S(1)}, bf16[64,512]{1,0:T(8,128)(2,1)S(1)}, bf16[64,512]{1,0:T(8,128)(2,1)S(1)}, bf16[64,512]{1,0:T(8,128)(2,1)S(1)}) custom-call(s32[5]{0:T(128)S(1)} %copy-done.6, bf16[64,2048]{1,0:T(8,128)(2,1)S(1)} %owned.1.refs_0_, bf16[64,2048]{1,0:T(8,128)(2,1)S(1)} %collective-permute-done.41.refs_1_, ...), custom_call_target="tpu_custom_call" | custom-call | bytes 2359296 | tf_op jit(solution)/shard_map/newton/pallas_call | solution.py:114
  215.9 3.5 %collective-permute-done.50.refs_2_ = bf16[64,512]{1,0:T(8,128)(2,1)S(1)} collective-permute-done((bf16[64,512]{1,0:T(8,128)(2,1)S(1)}, bf16[64,512]{1,0:T(8,128)(2,1)S(1)}, u32[]{:S(2)}, u32[]{:S(2)}) %collective-permute-start.50) | collective-permute-done | bytes 65568 | tf_op jit(solution)/shard_map/ppermute | solution.py:837
  230.7 3.2 %collective-permute-done.61.refs_3_ = bf16[64,1536]{1,0:T(8,128)(2,1)S(1)} collective-permute-done((bf16[64,1536]{1,0:T(8,128)(2,1)S(1)}, bf16[64,1536]{1,0:T(8,128)(2,1)S(1)}, u32[]{:S(2)}, u32[]{:S(2)}) %collective-permute-start.61) | collective-permute-done | bytes 196640 | tf_op jit(solution)/shard_map/ppermute | solution.py:840
  239.5 5.4 %grads.1 = (f32[512,512]{1,0:T(8,128)}, f32[512,512]{1,0:T(8,128)}, f32[512,512]{1,0:T(8,128)}, f32[512,512]{1,0:T(8,128)}, f32[512,384]{1,0:T(8,128)}, /*index=...) custom-call(s32[5]{0:T(128)} %stack.19.seat, bf16[64,1536]{1,0:T(8,128)(2,1)} %copy-done.11, ...), custom_call_target="tpu_custom_call" | custom-call | bytes 11010048 | tf_op jit(solution)/shard_map/grads/pallas_call | solution.py:114
  245.0 4.8 %weights.1 = (f32[512,512]{1,0:T(8,128)}, f32[512,512]{1,0:T(8,128)}, f32[512,384]{1,0:T(8,128)}, f32[512,128]{1,0:T(8,128)}) custom-call(s32[5]{0:T(128)} %stack.19.seat, bf16[64,1536]{1,0:T(8,128)(2,1)} %copy-done.2, bf16[64,1536]{1,0:T(8,128)(2,1)} %collective-permute-done.59.refs_1_, bf16[64,1536]{1,0:T(8,128)(2,1)} %copy-done.22, ...), custom_call_target="tpu_custom_call" | custom-call | bytes 7864320 | tf_op jit(solution)/shard_map/weights/pallas_call | solution.py:114
  (186 shorter events, 85.5 us)
Async XLA Ops:
  19.1 19.6 %collective-permute-start.9 = (bf16[192,512]{1,0:T(8,128)(2,1)S(1)}, bf16[192,512]{1,0:T(8,128)(2,1)S(1)}, u32[]{:S(2)}, u32[]{:S(2)}) collective-permute-start(bf16[192,512]{1,0:T(8,128)(2,1)S(1)} %far_qkv.1.refs_7_), channel_id=1, source_target_pairs={{0,4},{4,0},{8,12},{12,8},{16,20},{20,16},{24,28},{28,24},{1,5},{5... | collective-permute-start | bytes 589832 | tf_op jit(solution)/shard_map/ppermute | solution.py:840
  23.7 15.6 %collective-permute-start.8 = (bf16[192,512]{1,0:T(8,128)(2,1)S(1)}, bf16[192,512]{1,0:T(8,128)(2,1)S(1)}, u32[]{:S(2)}, u32[]{:S(2)}) collective-permute-start(bf16[192,512]{1,0:T(8,128)(2,1)S(1)} %far_qkv.1.refs_7_), channel_id=1, source_target_pairs={{0,24},{4,28},{8,16},{12,20},{16,8},{20,12},{24,0},{28,4},{1,25},{... | collective-permute-start | bytes 589832 | tf_op jit(solution)/shard_map/ppermute | solution.py:840
  35.7 24.8 %collective-permute-start.15 = (bf16[192,1024]{1,0:T(8,128)(2,1)S(1)}, bf16[192,1024]{1,0:T(8,128)(2,1)S(1)}, u32[]{:S(2)}, u32[]{:S(2)}) collective-permute-start(bf16[192,1024]{1,0:T(8,128)(2,1)S(1)} %far_up.1.refs_6_), channel_id=1, source_target_pairs={{0,24},{4,28},{8,16},{12,20},{16,8},{20,12},{24,0},{28,4},{1,25},{... | collective-permute-start | bytes 1179656 | tf_op jit(solution)/shard_map/ppermute | solution.py:840
  38.2 22.4 %collective-permute-start.14 = (bf16[192,1024]{1,0:T(8,128)(2,1)S(1)}, bf16[192,1024]{1,0:T(8,128)(2,1)S(1)}, u32[]{:S(2)}, u32[]{:S(2)}) collective-permute-start(bf16[192,1024]{1,0:T(8,128)(2,1)S(1)} %far_up.1.refs_6_), channel_id=1, source_target_pairs={{0,16},{4,20},{8,24},{12,28},{16,0},{20,4},{24,8},{28,12},{1,17},{... | collective-permute-start | bytes 1179656 | tf_op jit(solution)/shard_map/ppermute | solution.py:840
  38.7 22.3 %collective-permute-start.13 = (bf16[192,1024]{1,0:T(8,128)(2,1)S(1)}, bf16[192,1024]{1,0:T(8,128)(2,1)S(1)}, u32[]{:S(2)}, u32[]{:S(2)}) collective-permute-start(bf16[192,1024]{1,0:T(8,128)(2,1)S(1)} %far_up.1.refs_6_), channel_id=1, source_target_pairs={{0,8},{4,12},{8,0},{12,4},{16,24},{20,28},{24,16},{28,20},{1,9},{5... | collective-permute-start | bytes 1179656 | tf_op jit(solution)/shard_map/ppermute | solution.py:840
  39.2 20.7 %collective-permute-start.6 = (bf16[192,512]{1,0:T(8,128)(2,1)S(1)}, bf16[192,512]{1,0:T(8,128)(2,1)S(1)}, u32[]{:S(2)}, u32[]{:S(2)}) collective-permute-start(bf16[192,512]{1,0:T(8,128)(2,1)S(1)} %far_qkv.1.refs_7_), channel_id=1, source_target_pairs={{0,8},{4,12},{8,0},{12,4},{16,24},{20,28},{24,16},{28,20},{1,9},{5... | collective-permute-start | bytes 589832 | tf_op jit(solution)/shard_map/ppermute | solution.py:840
  40.7 19.2 %collective-permute-start.12 = (bf16[192,512]{1,0:T(8,128)(2,1)S(1)}, bf16[192,512]{1,0:T(8,128)(2,1)S(1)}, u32[]{:S(2)}, u32[]{:S(2)}) collective-permute-start(bf16[192,512]{1,0:T(8,128)(2,1)S(1)} %collective-permute-done.8.refs_10_), channel_id=1, source_target_pairs={{0,4},{4,0},{8,12},{12,8},{16,20},{20,16},{24,28},{28,24},{1,5},{5... | collective-permute-start | bytes 589832 | tf_op jit(solution)/shard_map/ppermute | solution.py:840
  60.0 18.3 %collective-permute-start.16 = (bf16[192,1024]{1,0:T(8,128)(2,1)S(1)}, bf16[192,1024]{1,0:T(8,128)(2,1)S(1)}, u32[]{:S(2)}, u32[]{:S(2)}) collective-permute-start(bf16[192,1024]{1,0:T(8,128)(2,1)S(1)} %far_up.1.refs_6_), channel_id=1, source_target_pairs={{0,4},{4,0},{8,12},{12,8},{16,20},{20,16},{24,28},{28,24},{1,5},{5... | collective-permute-start | bytes 1179656 | tf_op jit(solution)/shard_map/ppermute | solution.py:840
  60.5 17.8 %collective-permute-start.19 = (bf16[192,1024]{1,0:T(8,128)(2,1)S(1)}, bf16[192,1024]{1,0:T(8,128)(2,1)S(1)}, u32[]{:S(2)}, u32[]{:S(2)}) collective-permute-start(bf16[192,1024]{1,0:T(8,128)(2,1)S(1)} %collective-permute-done.15.refs_9_), channel_id=1, source_target_pairs={{0,4},{4,0},{8,12},{12,8},{16,20},{20,16},{24,28},{28,24},{1,5},{5... | collective-permute-start | bytes 1179656 | tf_op jit(solution)/shard_map/ppermute | solution.py:840
  60.5 17.7 %collective-permute-start.18 = (bf16[192,1024]{1,0:T(8,128)(2,1)S(1)}, bf16[192,1024]{1,0:T(8,128)(2,1)S(1)}, u32[]{:S(2)}, u32[]{:S(2)}) collective-permute-start(bf16[192,1024]{1,0:T(8,128)(2,1)S(1)} %collective-permute-done.14.refs_8_), channel_id=1, source_target_pairs={{0,4},{4,0},{8,12},{12,8},{16,20},{20,16},{24,28},{28,24},{1,5},{5... | collective-permute-start | bytes 1179656 | tf_op jit(solution)/shard_map/ppermute | solution.py:840
  61.0 17.3 %collective-permute-start.17 = (bf16[192,1024]{1,0:T(8,128)(2,1)S(1)}, bf16[192,1024]{1,0:T(8,128)(2,1)S(1)}, u32[]{:S(2)}, u32[]{:S(2)}) collective-permute-start(bf16[192,1024]{1,0:T(8,128)(2,1)S(1)} %collective-permute-done.13.refs_7_), channel_id=1, source_target_pairs={{0,4},{4,0},{8,12},{12,8},{16,20},{20,16},{24,28},{28,24},{1,5},{5... | collective-permute-start | bytes 1179656 | tf_op jit(solution)/shard_map/ppermute | solution.py:840
  112.6 14.8 %collective-permute-start.26 = (bf16[64,4096]{1,0:T(8,128)(2,1)S(1)}, bf16[64,4096]{1,0:T(8,128)(2,1)S(1)}, u32[]{:S(2)}, u32[]{:S(2)}) collective-permute-start(bf16[64,4096]{1,0:T(8,128)(2,1)S(1)} %get-tuple-element.171), channel_id=1, source_target_pairs={{0,8},{4,12},{8,0},{12,4},{16,24},{20,28},{24,16},{28,20},{1,9},{5... | collective-permute-start | bytes 1572872 | tf_op jit(solution)/shard_map/ppermute | solution.py:840
  114.1 26.0 %collective-permute-start.27 = (bf16[64,4096]{1,0:T(8,128)(2,1)S(1)}, bf16[64,4096]{1,0:T(8,128)(2,1)S(1)}, u32[]{:S(2)}, u32[]{:S(2)}) collective-permute-start(bf16[64,4096]{1,0:T(8,128)(2,1)S(1)} %get-tuple-element.172), channel_id=1, source_target_pairs={{0,16},{4,20},{8,24},{12,28},{16,0},{20,4},{24,8},{28,12},{1,17},{... | collective-permute-start | bytes 1572872 | tf_op jit(solution)/shard_map/ppermute | solution.py:840
  114.6 25.5 %collective-permute-start.28 = (bf16[64,4096]{1,0:T(8,128)(2,1)S(1)}, bf16[64,4096]{1,0:T(8,128)(2,1)S(1)}, u32[]{:S(2)}, u32[]{:S(2)}) collective-permute-start(bf16[64,4096]{1,0:T(8,128)(2,1)S(1)} %get-tuple-element.173), channel_id=1, source_target_pairs={{0,24},{4,28},{8,16},{12,20},{16,8},{20,12},{24,0},{28,4},{1,25},{... | collective-permute-start | bytes 1572872 | tf_op jit(solution)/shard_map/ppermute | solution.py:840
  117.0 28.4 %collective-permute-start.32 = (bf16[64,2048]{1,0:T(8,128)(2,1)S(1)}, bf16[64,2048]{1,0:T(8,128)(2,1)S(1)}, u32[]{:S(2)}, u32[]{:S(2)}) collective-permute-start(bf16[64,2048]{1,0:T(8,128)(2,1)S(1)} %get-tuple-element.179), channel_id=1, source_target_pairs={{0,8},{4,12},{8,0},{12,4},{16,24},{20,28},{24,16},{28,20},{1,9},{5... | collective-permute-start | bytes 786440 | tf_op jit(solution)/shard_map/ppermute | solution.py:840
  118.6 31.9 %collective-permute-start.33 = (bf16[64,2048]{1,0:T(8,128)(2,1)S(1)}, bf16[64,2048]{1,0:T(8,128)(2,1)S(1)}, u32[]{:S(2)}, u32[]{:S(2)}) collective-permute-start(bf16[64,2048]{1,0:T(8,128)(2,1)S(1)} %get-tuple-element.180), channel_id=1, source_target_pairs={{0,16},{4,20},{8,24},{12,28},{16,0},{20,4},{24,8},{28,12},{1,17},{... | collective-permute-start | bytes 786440 | tf_op jit(solution)/shard_map/ppermute | solution.py:840
  127.4 23.5 %collective-permute-start.34 = (bf16[64,2048]{1,0:T(8,128)(2,1)S(1)}, bf16[64,2048]{1,0:T(8,128)(2,1)S(1)}, u32[]{:S(2)}, u32[]{:S(2)}) collective-permute-start(bf16[64,2048]{1,0:T(8,128)(2,1)S(1)} %get-tuple-element.181), channel_id=1, source_target_pairs={{0,24},{4,28},{8,16},{12,20},{16,8},{20,12},{24,0},{28,4},{1,25},{... | collective-permute-start | bytes 786440 | tf_op jit(solution)/shard_map/ppermute | solution.py:840
  142.6 15.4 %collective-permute-start.30 = (bf16[64,1024]{1,0:T(8,128)(2,1)S(1)}, bf16[64,1024]{1,0:T(8,128)(2,1)S(1)}, u32[]{:S(2)}, u32[]{:S(2)}) collective-permute-start(bf16[64,1024]{1,0:T(8,128)(2,1)S(1)} %get-tuple-element.176), channel_id=1, source_target_pairs={{0,2},{1,3},{2,0},{3,1},{4,6},{5,7},{6,4},{7,5},{8,10},{9,11},{10,... | collective-permute-start | bytes 393224 | tf_op jit(solution)/shard_map/ppermute | solution.py:837
  178.0 15.6 %collective-permute-start.44 = (bf16[64,2048]{1,0:T(8,128)(2,1)S(1)}, bf16[64,2048]{1,0:T(8,128)(2,1)S(1)}, u32[]{:S(2)}, u32[]{:S(2)}) collective-permute-start(bf16[64,2048]{1,0:T(8,128)(2,1)S(1)} %owned.1.refs_0_), channel_id=1, source_target_pairs={{0,4},{4,0},{8,12},{12,8},{16,20},{20,16},{24,28},{28,24},{1,5},{5... | collective-permute-start | bytes 786440 | tf_op jit(solution)/shard_map/ppermute | solution.py:840
  191.9 20.6 %collective-permute-start.48 = (f32[28,512]{1,0:T(8,128)S(1)}, f32[28,512]{1,0:T(8,128)S(1)}, u32[]{:S(2)}, u32[]{:S(2)}) collective-permute-start(f32[28,512]{1,0:T(8,128)S(1)} %add.7.refs_0_), channel_id=1, source_target_pairs={{0,2},{1,3},{2,0},{3,1},{4,6},{5,7},{6,4},{7,5},{8,10},{9,11},{10,... | collective-permute-start | bytes 172040 | tf_op jit(solution)/shard_map/ppermute | solution.py:837
  210.3 17.7 %collective-permute-start.55 = (bf16[64,1536]{1,0:T(8,128)(2,1)S(1)}, bf16[64,1536]{1,0:T(8,128)(2,1)}, u32[]{:S(2)}, u32[]{:S(2)}) collective-permute-start(bf16[64,1536]{1,0:T(8,128)(2,1)S(1)} %get-tuple-element.203.refs_0_), channel_id=1, source_target_pairs={{0,4},{4,0},{8,12},{12,8},{16,20},{20,16},{24,28},{28,24},{1,5},{5... | collective-permute-start | bytes 589832 | tf_op jit(solution)/shard_map/ppermute | solution.py:840
  210.3 18.7 %collective-permute-start.54 = (bf16[64,1536]{1,0:T(8,128)(2,1)S(1)}, bf16[64,1536]{1,0:T(8,128)(2,1)}, u32[]{:S(2)}, u32[]{:S(2)}) collective-permute-start(bf16[64,1536]{1,0:T(8,128)(2,1)S(1)} %get-tuple-element.203.refs_0_), channel_id=1, source_target_pairs={{0,24},{4,28},{8,16},{12,20},{16,8},{20,12},{24,0},{28,4},{1,25},{... | collective-permute-start | bytes 589832 | tf_op jit(solution)/shard_map/ppermute | solution.py:840
  211.4 18.8 %collective-permute-start.53 = (bf16[64,1536]{1,0:T(8,128)(2,1)S(1)}, bf16[64,1536]{1,0:T(8,128)(2,1)}, u32[]{:S(2)}, u32[]{:S(2)}) collective-permute-start(bf16[64,1536]{1,0:T(8,128)(2,1)S(1)} %get-tuple-element.203.refs_0_), channel_id=1, source_target_pairs={{0,16},{4,20},{8,24},{12,28},{16,0},{20,4},{24,8},{28,12},{1,17},{... | collective-permute-start | bytes 589832 | tf_op jit(solution)/shard_map/ppermute | solution.py:840
  212.5 17.8 %collective-permute-start.52 = (bf16[64,1536]{1,0:T(8,128)(2,1)S(1)}, bf16[64,1536]{1,0:T(8,128)(2,1)}, u32[]{:S(2)}, u32[]{:S(2)}) collective-permute-start(bf16[64,1536]{1,0:T(8,128)(2,1)S(1)} %get-tuple-element.203.refs_0_), channel_id=1, source_target_pairs={{0,8},{4,12},{8,0},{12,4},{16,24},{20,28},{24,16},{28,20},{1,9},{5... | collective-permute-start | bytes 589832 | tf_op jit(solution)/shard_map/ppermute | solution.py:840
  (66 other events, 1009.7 us)
